TPU v7x, 512 devices: a whole 4x8x8 slice. The times are simulated.
512 devices in a mesh: subj: 32 (over z, y_lo), slab: 16 (over y_hi, x, core).
Axes of the slice: x: 4, y: 8 (y_hi: 2, y_lo: 4; y = y_hi * 4 + y_lo), z: 8, core: 2. Of those that a mesh axis runs over, the one named last changes fastest.
Arguments:
- data_rhs: float32 [32, 16, 64, 1536], P('subj', None, 'slab'), may hold values from -12 to 12
- inv_var: float32 [32, 64, 1536], P('subj', 'slab'), may hold values from 0.01 to 0.3
- design: float32 [32, 16], P('subj'), may hold values from 0.5 to 4
- keep_mask: int32 [32, 64, 1536], P('subj', 'slab'), may hold values 0 or 1
- brain_mask: int32 [64, 1536], P('slab'), may hold values 0 or 1
- tissue: int32 [64, 1536], P('slab'), may hold values from 0 to 2
- kappa_sq: float32 [3, 16], replicated, may hold values from 0.005 to 0.5
- prior_scale: float32 [16], replicated, may hold values from 0.5 to 2
- mean_field: float32 [16, 64, 1536], P(None, 'slab', 'subj'), may hold values from -6 to 6
- pop_noise: float32 [16, 64, 1536], P(None, 'slab', 'subj'), may hold values from -6 to 6
Outputs:
- subject_fields: float32 [32, 16, 64, 1536], P('subj', None, 'slab')
- new_mean: float32 [16, 64, 1536], P(None, 'slab', 'subj')
All inputs are finite; a program needn't handle non-finite values. No bound on the sum of `keep_mask` or of `brain_mask` on one device may be relied on, other than what follows from the above.
Results may differ from a plain program's by a relative error of at most 0.00016.
Values sent between devices are 32-bit elements; how exact they have to be, the bound alone decides.
A program may use at most 64 MiB of HBM per device.

v0:
```python
import math

import jax
import jax.numpy as jnp
from jax import lax
from jax.sharding import PartitionSpec as P

CLASSES = 3
ITERS = 8
CX = 64


MEAN_PRECISION = 1.0


def padded_2(cells, sides, width):
    for axis, dim in sides:
        count = lax.axis_size(axis)
        ends = count - 1
        head = lax.slice_in_dim(cells, 0, width, axis=dim)
        tail = lax.slice_in_dim(cells, cells.shape[dim] - width, cells.shape[dim], axis=dim)
        cells = jnp.concatenate(
            [
                lax.ppermute(tail, axis, [(i, (i + 1) % count) for i in range(ends)]),
                cells,
                lax.ppermute(head, axis, [((i + 1) % count, i) for i in range(ends)]),
            ],
            axis=dim,
        )
    return cells


def plane_beside(center):
    cells = center.shape[-1]
    column = lax.iota(jnp.int32, cells) % CX
    zeros_one = jnp.zeros(center.shape[:-1] + (1,), jnp.float32)
    zeros_row = jnp.zeros(center.shape[:-1] + (CX,), jnp.float32)
    from_left = jnp.where(column > 0, jnp.concatenate([zeros_one, center[..., :-1]], axis=-1), 0.0)
    from_right = jnp.where(
        column < CX - 1, jnp.concatenate([center[..., 1:], zeros_one], axis=-1), 0.0
    )
    from_below = jnp.concatenate([zeros_row, center[..., :-CX]], axis=-1)
    from_above = jnp.concatenate([center[..., CX:], zeros_row], axis=-1)
    return from_left + from_right + from_below + from_above


def beside_of(padded):
    center = padded[:, :, 1:-1]
    return padded[:, :, 2:] + padded[:, :, :-2] + plane_beside(center)


def local(
    data_rhs,
    inv_var,
    design,
    keep_mask,
    brain_mask,
    tissue,
    kappa_sq,
    prior_scale,
    mean_field,
    pop_noise,
):
    in_brain = brain_mask.astype(jnp.float32)
    kappa_field = jnp.zeros((prior_scale.shape[0],) + tissue.shape, jnp.float32)
    for label in range(CLASSES):
        kappa_field = (
            kappa_field
            + jnp.where(tissue == label, 1.0, 0.0)[None] * kappa_sq[label][:, None, None]
        )
    scale_col = prior_scale[:, None, None]
    shifted = 6.0 + kappa_field
    whole_mean = lax.all_gather(mean_field, "subj", axis=2, tiled=True)
    padded_mean = padded_2(whole_mean[None], (("slab", 2),), 1)
    prior_mean = scale_col * (shifted * padded_mean[:, :, 1:-1] - beside_of(padded_mean))
    voxel_factor = inv_var * in_brain * keep_mask.astype(jnp.float32)
    diagonal = design[:, :, None, None] * voxel_factor[:, None] + scale_col * shifted
    right_side = data_rhs + prior_mean

    def inner(left, right):
        return jnp.sum(left * right, axis=(2, 3))

    solution = jnp.zeros_like(right_side)
    residual = right_side

    def residual_norm(current):
        local_norm = inner(current, current)
        return lax.psum(local_norm, "slab")

    direction = right_side
    norm_now = residual_norm(residual)
    for iteration in range(ITERS):
        applied = diagonal * direction - scale_col * beside_of(
            padded_2(direction, (("slab", 2),), 1)
        )
        local_curv = inner(direction, applied)
        curv_sum = lax.psum(local_curv, "slab")
        step_size = norm_now / curv_sum
        solution = solution + step_size[:, :, None, None] * direction
        if iteration + 1 < ITERS:
            residual = residual - step_size[:, :, None, None] * applied
            norm_next = residual_norm(residual)
            direction = residual + (norm_next / norm_now)[:, :, None, None] * direction
            norm_now = norm_next
    subject_total = jnp.sum(solution, axis=0)
    summed = lax.psum_scatter(subject_total, "subj", scatter_dimension=2, tiled=True)
    subjects = design.shape[0] * lax.axis_size("subj")
    divisor = subjects + MEAN_PRECISION
    new_mean = summed / divisor + pop_noise / math.sqrt(divisor)
    return (solution, new_mean)


def solution(mesh):
    in_specs = (
        P("subj", None, "slab", None),
        P("subj", "slab", None),
        P("subj", None),
        P("subj", "slab", None),
        P("slab", None),
        P("slab", None),
        P(),
        P(),
        P(None, "slab", "subj"),
        P(None, "slab", "subj"),
    )
    out_specs = (P("subj", None, "slab", None), P(None, "slab", "subj"))
    return jax.shard_map(local, mesh=mesh, in_specs=in_specs, out_specs=out_specs, check_vma=False)
```

profile of v0, /device:TPU:6, one launch (start us, length us, event | category | flops | bytes accessed | tf_op | source)
XLA Modules:
  0.0 1116.8 jit_solution(7056748842792953106)
XLA Ops:
  8.1 126.5 %all_gather.3 = f32[16,4,1536]{0,1,2:T(4,128)} all-gather(f32[16,4,48]{0,1,2:T(4,128)S(1)} %copy.79), channel_id=1, replica_groups=mesh['subj'=32,'slab'=16] {'subj'}, dimensions={2}, use_global_device_ids=true | all-gather | bytes 405504 | tf_op jit(solution)/shard_map/all_gather | solution.py:73
  151.8 3.7 collective-permute-done.3
  156.1 47.8 %all-reduce.36 = (f32[1,16]{1,0:T(1,128)S(1)}, f32[1,16]{1,0:T(1,128)S(1)}) all-reduce(f32[1,16]{1,0:T(1,128)S(1)} %bitcast.85, f32[1,16]{1,0:T(1,128)S(1)} %bitcast.84), channel_id=1, replica_groups=mesh['subj'=32,'slab'=16] {'slab'}, use_global_device_ids=true, to_apply=%region_1.2 | all-reduce | flops 32 | bytes 256 | tf_op jit(solution)/shard_map/psum | solution.py:88
  204.1 42.8 %psum.114 = f32[1,16]{1,0:T(1,128)S(1)} all-reduce(f32[1,16]{1,0:T(1,128)S(1)} %bitcast.90), channel_id=1, replica_groups=mesh['subj'=32,'slab'=16] {'slab'}, use_global_device_ids=true, to_apply=%region_5.6 | all-reduce | flops 16 | bytes 128 | tf_op jit(solution)/shard_map/psum | solution.py:88
  256.4 48.8 %psum.115 = f32[1,16]{1,0:T(1,128)S(1)} all-reduce(f32[1,16]{1,0:T(1,128)S(1)} %bitcast.92), channel_id=1, replica_groups=mesh['subj'=32,'slab'=16] {'slab'}, use_global_device_ids=true, to_apply=%region_7.8 | all-reduce | flops 16 | bytes 128 | tf_op jit(solution)/shard_map/psum | solution.py:97
  306.8 42.8 %psum.116 = f32[1,16]{1,0:T(1,128)S(1)} all-reduce(f32[1,16]{1,0:T(1,128)S(1)} %bitcast.82), channel_id=1, replica_groups=mesh['subj'=32,'slab'=16] {'slab'}, use_global_device_ids=true, to_apply=%region_9.10 | all-reduce | flops 16 | bytes 128 | tf_op jit(solution)/shard_map/psum | solution.py:88
  359.6 48.8 %psum.117 = f32[1,16]{1,0:T(1,128)S(1)} all-reduce(f32[1,16]{1,0:T(1,128)S(1)} %bitcast.93), channel_id=1, replica_groups=mesh['subj'=32,'slab'=16] {'slab'}, use_global_device_ids=true, to_apply=%region_11.12 | all-reduce | flops 16 | bytes 128 | tf_op jit(solution)/shard_map/psum | solution.py:97
  409.3 42.8 %psum.118 = f32[1,16]{1,0:T(1,128)S(1)} all-reduce(f32[1,16]{1,0:T(1,128)S(1)} %bitcast.86), channel_id=1, replica_groups=mesh['subj'=32,'slab'=16] {'slab'}, use_global_device_ids=true, to_apply=%region_13.14 | all-reduce | flops 16 | bytes 128 | tf_op jit(solution)/shard_map/psum | solution.py:88
  457.6 3.3 collective-permute-done.9
  462.1 48.8 %psum.119 = f32[1,16]{1,0:T(1,128)S(1)} all-reduce(f32[1,16]{1,0:T(1,128)S(1)} %bitcast.94), channel_id=1, replica_groups=mesh['subj'=32,'slab'=16] {'slab'}, use_global_device_ids=true, to_apply=%region_15.16 | all-reduce | flops 16 | bytes 128 | tf_op jit(solution)/shard_map/psum | solution.py:97
  511.8 42.8 %psum.120 = f32[1,16]{1,0:T(1,128)S(1)} all-reduce(f32[1,16]{1,0:T(1,128)S(1)} %bitcast.87), channel_id=1, replica_groups=mesh['subj'=32,'slab'=16] {'slab'}, use_global_device_ids=true, to_apply=%region_17.18 | all-reduce | flops 16 | bytes 128 | tf_op jit(solution)/shard_map/psum | solution.py:88
  560.2 3.3 collective-permute-done.11
  564.6 48.8 %psum.121 = f32[1,16]{1,0:T(1,128)S(1)} all-reduce(f32[1,16]{1,0:T(1,128)S(1)} %bitcast.95), channel_id=1, replica_groups=mesh['subj'=32,'slab'=16] {'slab'}, use_global_device_ids=true, to_apply=%region_19.20 | all-reduce | flops 16 | bytes 128 | tf_op jit(solution)/shard_map/psum | solution.py:97
  614.3 42.8 %psum.122 = f32[1,16]{1,0:T(1,128)S(1)} all-reduce(f32[1,16]{1,0:T(1,128)S(1)} %bitcast.88), channel_id=1, replica_groups=mesh['subj'=32,'slab'=16] {'slab'}, use_global_device_ids=true, to_apply=%region_21.22 | all-reduce | flops 16 | bytes 128 | tf_op jit(solution)/shard_map/psum | solution.py:88
  662.7 3.3 collective-permute-done.13
  667.2 48.8 %psum.123 = f32[1,16]{1,0:T(1,128)S(1)} all-reduce(f32[1,16]{1,0:T(1,128)S(1)} %bitcast.96), channel_id=1, replica_groups=mesh['subj'=32,'slab'=16] {'slab'}, use_global_device_ids=true, to_apply=%region_23.24 | all-reduce | flops 16 | bytes 128 | tf_op jit(solution)/shard_map/psum | solution.py:97
  717.5 42.9 %psum.124 = f32[1,16]{1,0:T(1,128)S(1)} all-reduce(f32[1,16]{1,0:T(1,128)} %bitcast.89), channel_id=1, replica_groups=mesh['subj'=32,'slab'=16] {'slab'}, use_global_device_ids=true, to_apply=%region_25.26 | all-reduce | flops 16 | bytes 128 | tf_op jit(solution)/shard_map/psum | solution.py:88
  765.9 3.3 collective-permute-done.15
  771.0 49.5 %psum.125 = f32[1,16]{1,0:T(1,128)} all-reduce(f32[1,16]{1,0:T(1,128)} %bitcast.97), channel_id=1, replica_groups=mesh['subj'=32,'slab'=16] {'slab'}, use_global_device_ids=true, to_apply=%region_27.28 | all-reduce | flops 16 | bytes 128 | tf_op jit(solution)/shard_map/psum | solution.py:97
  822.5 43.4 %psum.126 = f32[1,16]{1,0:T(1,128)} all-reduce(f32[1,16]{1,0:T(1,128)} %bitcast.91), channel_id=1, replica_groups=mesh['subj'=32,'slab'=16] {'slab'}, use_global_device_ids=true, to_apply=%region_29.30 | all-reduce | flops 16 | bytes 128 | tf_op jit(solution)/shard_map/psum | solution.py:88
  877.6 49.1 %psum.127 = f32[1,16]{1,0:T(1,128)S(1)} all-reduce(f32[1,16]{1,0:T(1,128)} %bitcast.83), channel_id=1, replica_groups=mesh['subj'=32,'slab'=16] {'slab'}, use_global_device_ids=true, to_apply=%region_31.32 | all-reduce | flops 16 | bytes 128 | tf_op jit(solution)/shard_map/psum | solution.py:97
  928.4 8.3 copy.85
  936.7 9.8 reshape.112
  947.6 160.5 %reduce-scatter.4.cloned.1.call-done = f32[48,64]{1,0:T(8,128)} async-done(((f32[1536,64]{1,0:T(8,128)}), f32[48,64]{1,0:T(8,128)}) %reduce-scatter.4.cloned.1.call-update) | async-done | bytes 12304
  (153 shorter events, 89.6 us)
Async XLA Ops:
  7.2 1100.9 %reduce-scatter.4.cloned.1.call-start = ((), (), s32[]{:S(2)}) async-start(), calls=%async_computation.1 | async-start | bytes 811008
  137.7 7.1 collective-permute-start
  139.6 5.9 collective-permute-start.1
  144.0 522.0 %copy-start.1 = (f32[4,1536]{1,0:T(4,128)}, f32[4,1536]{1,0:T(4,128)S(1)}, u32[]{:S(2)}) copy-start(f32[4,1536]{1,0:T(4,128)S(1)} %get-tuple-element.89) | copy-start | bytes 73732
  144.0 522.0 %copy-start.2 = (f32[4,1536]{1,0:T(4,128)}, f32[4,1536]{1,0:T(4,128)S(1)}, u32[]{:S(2)}) copy-start(f32[4,1536]{1,0:T(4,128)S(1)} %get-tuple-element.90) | copy-start | bytes 73732
  144.0 522.0 %copy-start.3 = (f32[4,1536]{1,0:T(4,128)}, f32[4,1536]{1,0:T(4,128)S(1)}, u32[]{:S(2)}) copy-start(f32[4,1536]{1,0:T(4,128)S(1)} %get-tuple-element.91) | copy-start | bytes 73732
  144.8 521.2 %copy-start.4 = (f32[4,1536]{1,0:T(4,128)}, f32[4,1536]{1,0:T(4,128)S(1)}, u32[]{:S(2)}) copy-start(f32[4,1536]{1,0:T(4,128)S(1)} %fusion.40) | copy-start | bytes 73732
  147.2 4.6 collective-permute-start.2
  149.6 5.9 collective-permute-start.3
  247.4 4.6 collective-permute-start.4
  249.3 5.9 collective-permute-start.5
  350.5 4.6 collective-permute-start.6
  352.4 5.9 collective-permute-start.7
  453.0 4.6 collective-permute-start.8
  455.0 5.9 collective-permute-start.9
  555.6 4.6 collective-permute-start.10
  557.5 5.9 collective-permute-start.11
  658.1 4.6 collective-permute-start.12
  660.0 5.9 collective-permute-start.13
  761.3 4.6 collective-permute-start.14
  763.2 5.9 collective-permute-start.15
  867.9 4.6 collective-permute-start.16
  869.8 5.9 collective-permute-start.17
  928.4 180.9 %copy-start.7 = (f32[16,4,48]{2,1,0:T(4,128)S(1)}, f32[16,4,48]{2,1,0:T(4,128)}, u32[]{:S(2)}) copy-start(f32[16,4,48]{2,1,0:T(4,128)} %param.19) | copy-start | bytes 36868
  (17 other events, 737.8 us)
Sparse Core Ops, SparseCore 0:
  946.7 161.3 reduce-scatter.3
where the time goes:
time: 1120 us
  blocking collectives  817 us (73%)
  waiting for transfers between devices  188 us (17%)
  starting transfers between devices  39.6 us (4%)
  local copies, waits for them, and re-layouts  29 us (3%)
  other arithmetic  28.6 us (3%)
  between operations  14.6 us (1%)
    psum x8, blocking collectives, residual_norm(): return lax.psum(local_norm, 'slab')  348 us
    psum x7, blocking collectives, local(): curv_sum = lax.psum(local_curv, 'slab')  343 us
    unnamed x2, waiting for transfers between devices  161 us
    all_gather x1, blocking collectives, local(): whole_mean = lax.all_gather(mean_field, 'subj', axis=2, tiled=True)  127 us
    ppermute x9, waiting for transfers between devices, padded_2(): lax.ppermute(tail, axis, [(i, (i + 1) % count) for i in range(ends)])  27.4 us
  transfers between devices with their start and end apart: 19, of which 10 were waited for; matrix products, arithmetic and copies ran while one was open for 0% of the time, Pallas kernels for 0%

commit v1 on v0

v1 whole, which is shorter than its diff:
```python
import math

import jax
import jax.numpy as jnp
from jax import lax
from jax.experimental import pallas as pl
from jax.experimental.pallas import tpu as pltpu
from jax.sharding import PartitionSpec as P

ITERS = 8
CX = 64
LANES = 128
MEAN_PRECISION = 1.0


def tiles_of(ref, row, columns):
    return [ref[row : row + 8, LANES * t : LANES * (t + 1)] for t in range(columns)]


def beside_tiles(ref, block, columns):
    lane = lax.broadcasted_iota(jnp.int32, (8, LANES), 1)
    column = lane % CX
    has_left = column > 0
    has_right = column < CX - 1
    low = lane < CX
    row = 8 + 8 * block
    center = tiles_of(ref, row, columns)
    before = tiles_of(ref, row - 1, columns)
    after = tiles_of(ref, row + 1, columns)
    swapped = [pltpu.roll(tile, CX, 1) for tile in center]
    zero = jnp.zeros((8, LANES), jnp.float32)
    sums = []
    for t in range(columns):
        left = jnp.where(has_left, pltpu.roll(center[t], 1, 1), 0.0)
        right = jnp.where(has_right, pltpu.roll(center[t], LANES - 1, 1), 0.0)
        prev_half = swapped[t - 1] if t else zero
        next_half = swapped[t + 1] if t + 1 < columns else zero
        rows = swapped[t] + jnp.where(low, prev_half, next_half)
        sums.append((left + right) + rows + (before[t] + after[t]))
    return center, sums


def total(parts):
    while len(parts) > 1:
        parts = [
            parts[i] + parts[i + 1] if i + 1 < len(parts) else parts[i]
            for i in range(0, len(parts), 2)
        ]
    return jnp.sum(parts[0], axis=(0, 1), keepdims=True)


def solve_kernel(
    design, kappa, scale_ref, rhs, factor, tissue, mean, out, direction, padded_mean, residual,
    applied, diagonal,
):
    regressor = lax.axis_index("slab")
    planes, cells = out.shape
    columns = cells // LANES
    blocks = planes // 8
    design_k = design[0, regressor]
    scale = scale_ref[regressor]
    edge = jnp.zeros((8, cells), jnp.float32)
    for ref in (direction, padded_mean):
        ref[0:8, :] = edge
        ref[8 + planes : 16 + planes, :] = edge
    padded_mean[8 : 8 + planes, :] = mean[...]
    norms = []
    for block in range(blocks):
        center, sums = beside_tiles(padded_mean, block, columns)
        for t in range(columns):
            at = (slice(8 * block, 8 * block + 8), slice(LANES * t, LANES * (t + 1)))
            label = tissue[at]
            kappa_field = jnp.where(
                label == 0,
                kappa[0, regressor],
                jnp.where(label == 1, kappa[1, regressor], kappa[2, regressor]),
            )
            shifted = 6.0 + kappa_field
            right_side = rhs[at] + scale * (shifted * center[t] - sums[t])
            diagonal[at] = design_k * factor[at] + scale * shifted
            residual[at] = right_side
            direction[8 + 8 * block : 16 + 8 * block, at[1]] = right_side
            norms.append(right_side * right_side)
        norms = [sum(norms[1:], norms[0])]
    out[...] = jnp.zeros((planes, cells), jnp.float32)

    def step(iteration, norm_now):
        curvs = []
        for block in range(blocks):
            center, sums = beside_tiles(direction, block, columns)
            for t in range(columns):
                at = (slice(8 * block, 8 * block + 8), slice(LANES * t, LANES * (t + 1)))
                value = diagonal[at] * center[t] - scale * sums[t]
                applied[at] = value
                curvs.append(center[t] * value)
            curvs = [total_tile(curvs)]
        step_size = norm_now / total(curvs)
        norms = []
        for block in range(blocks):
            for t in range(columns):
                at = (slice(8 * block, 8 * block + 8), slice(LANES * t, LANES * (t + 1)))
                out[at] += step_size * direction[8 + 8 * block : 16 + 8 * block, at[1]]
                value = residual[at] - step_size * applied[at]
                residual[at] = value
                norms.append(value * value)
            norms = [total_tile(norms)]
        norm_next = total(norms)
        ratio = norm_next / norm_now
        for block in range(blocks):
            for t in range(columns):
                at = (slice(8 * block, 8 * block + 8), slice(LANES * t, LANES * (t + 1)))
                own = (slice(8 + 8 * block, 16 + 8 * block), at[1])
                direction[own] = residual[at] + ratio * direction[own]
        return norm_next

    def last(norm_now):
        curvs = []
        for block in range(blocks):
            center, sums = beside_tiles(direction, block, columns)
            for t in range(columns):
                at = (slice(8 * block, 8 * block + 8), slice(LANES * t, LANES * (t + 1)))
                curvs.append(center[t] * (diagonal[at] * center[t] - scale * sums[t]))
            curvs = [total_tile(curvs)]
        step_size = norm_now / total(curvs)
        for block in range(blocks):
            for t in range(columns):
                at = (slice(8 * block, 8 * block + 8), slice(LANES * t, LANES * (t + 1)))
                out[at] += step_size * direction[8 + 8 * block : 16 + 8 * block, at[1]]

    last(lax.fori_loop(0, ITERS - 1, step, total(norms)))


def total_tile(parts):
    while len(parts) > 1:
        parts = [
            parts[i] + parts[i + 1] if i + 1 < len(parts) else parts[i]
            for i in range(0, len(parts), 2)
        ]
    return parts[0]


def solve(design, kappa_sq, prior_scale, rhs, factor, tissue, mean):
    planes, cells = rhs.shape
    vmem = pl.BlockSpec(memory_space=pltpu.VMEM)
    smem = pl.BlockSpec(memory_space=pltpu.SMEM)
    field = pltpu.VMEM((planes, cells), jnp.float32)
    padded = pltpu.VMEM((planes + 16, cells), jnp.float32)
    return pl.pallas_call(
        solve_kernel,
        out_shape=jax.ShapeDtypeStruct((planes, cells), jnp.float32),
        in_specs=[smem] * 3 + [vmem] * 4,
        out_specs=vmem,
        scratch_shapes=[padded, padded, field, field, field],
        name="solve",
    )(design, kappa_sq, prior_scale, rhs, factor, tissue, mean)


def local(
    data_rhs,
    inv_var,
    design,
    keep_mask,
    brain_mask,
    tissue,
    kappa_sq,
    prior_scale,
    mean_field,
    pop_noise,
):
    slabs = lax.axis_size("slab")
    depth, cells = tissue.shape
    planes = slabs * depth
    factor = inv_var[0] * (brain_mask.astype(jnp.float32) * keep_mask[0].astype(jnp.float32))
    sent = jnp.stack([factor, tissue.astype(jnp.float32)])
    both = lax.all_gather(sent, "slab", axis=1, tiled=True)
    rhs = lax.all_to_all(data_rhs[0], "slab", 0, 0, tiled=True).reshape(planes, cells)
    mean = lax.all_to_all(mean_field, "slab", 0, 0, tiled=True).reshape(planes, -1)
    mean = lax.all_gather(mean, "subj", axis=1, tiled=True)
    fields = solve(design, kappa_sq, prior_scale, rhs, both[0], both[1], mean)
    back = lax.all_to_all(fields.reshape(slabs, depth, cells), "slab", 0, 0, tiled=True)
    summed = lax.psum_scatter(fields, "subj", scatter_dimension=1, tiled=True)
    summed = lax.all_to_all(summed.reshape(slabs, depth, -1), "slab", 0, 0, tiled=True)
    divisor = lax.axis_size("subj") + MEAN_PRECISION
    new_mean = summed / divisor + pop_noise / math.sqrt(divisor)
    return (back[None], new_mean)


def solution(mesh):
    in_specs = (
        P("subj", None, "slab", None),
        P("subj", "slab", None),
        P("subj", None),
        P("subj", "slab", None),
        P("slab", None),
        P("slab", None),
        P(),
        P(),
        P(None, "slab", "subj"),
        P(None, "slab", "subj"),
    )
    out_specs = (P("subj", None, "slab", None), P(None, "slab", "subj"))
    return jax.shard_map(local, mesh=mesh, in_specs=in_specs, out_specs=out_specs, check_vma=False)
```

time: 1120 us -> 355 us (0.32)
  the two profiles are of different devices: /device:TPU:6 before, /device:TPU:1 now
where the time goes in v1:
time: 355 us; the launch traced here: 354 us
  waiting for transfers between devices  137 us (39%)
  blocking collectives  113 us (32%)
  starting transfers between devices  65.9 us (19%)
  between operations  14.1 us (4%)
  local copies, waits for them, and re-layouts  13.3 us (4%)
  Pallas kernels  8.31 us (2%)
    unnamed x2, waiting for transfers between devices  127 us
    all_gather x1, blocking collectives, local(): mean = lax.all_gather(mean, 'subj', axis=1, tiled=True)  79.6 us
    all_gather x1, blocking collectives, local(): both = lax.all_gather(sent, 'slab', axis=1, tiled=True)  33.9 us
    all_to_all x1, starting transfers between devices, local(): lax.all_to_all(summed.reshape(slabs, depth, -1), 'slab', 0, 0, tiled=True)  30.9 us
    all_to_all x1, starting transfers between devices, local(): lax.all_to_all(fields.reshape(slabs, depth, cells), 'slab', 0, 0, tiled=T...  20.3 us
    all_to_all x1, starting transfers between devices, local(): lax.all_to_all(mean_field, 'slab', 0, 0, tiled=True).reshape(planes, -1)  11.2 us
    all_to_all x1, waiting for transfers between devices, local(): lax.all_to_all(summed.reshape(slabs, depth, -1), 'slab', 0, 0, tiled=True)  9.7 us
    unnamed x19, local copies, waits for them, and re-layouts  8.41 us
  transfers between devices with their start and end apart: 5, of which 2 were waited for; matrix products, arithmetic and copies ran while one was open for 2% of the time, Pallas kernels for 0%

profile of v1, /device:TPU:1, one launch (start us, length us, event | category | flops | bytes accessed | tf_op | source)
XLA Modules:
  0.0 354.2 jit_solution(15428665984365257838)
XLA Ops:
  7.2 1.5 reshape.23
  8.6 11.2 %all-to-all-start.1 = ((f32[16,1,192]{2,1,0:T(1,128)}), f32[16,1,192]{2,1,0:T(1,128)S(1)}, u32[]{:S(2)}, u32[]{:S(2)}) async-start(f32[16,1,192]{2,1,0:T(1,128)} %reshape.23), calls=%async_computation.1 | async-start | bytes 32768 | tf_op jit(solution)/shard_map/all_to_all | solution.py:177
  19.9 0.7 copy-done.5
  20.7 33.9 %all_gather.6 = f32[2,64,1536]{2,0,1:T(2,128)S(1)} all-gather(f32[2,4,1536]{2,0,1:T(2,128)S(1)} %pad_maximum_fusion), channel_id=1, replica_groups=mesh['subj'=32,'slab'=16] {'slab'}, dimensions={1}, use_global_device_ids=true | all-gather | bytes 835584 | tf_op jit(solution)/shard_map/all_gather | solution.py:175
  54.6 3.5 all-to-all-start
  58.1 0.6 fusion.1
  58.8 0.9 copy_bitcast_fusion
  60.9 79.6 %all_gather.7 = f32[64,1536]{0,1:T(8,128)S(1)} all-gather(f32[64,48]{0,1:T(8,128)S(1)} %copy.18), channel_id=1, replica_groups=mesh['subj'=32,'slab'=16] {'subj'}, dimensions={1}, use_global_device_ids=true | all-gather | bytes 405504 | tf_op jit(solution)/shard_map/all_gather | solution.py:178
  140.5 1.0 copy.19.mean
  141.5 0.9 reshape.17.rhs
  142.4 8.3 %solve.1 = f32[64,1536]{1,0:T(8,128)} custom-call(f32[1,16]{1,0:T(1,128)} %design.1, f32[3,16]{1,0:T(4,128)} %kappa.1, f32[16]{0:T(128)} %scale_ref.1, f32[64,1536]{1,0:T(8,128)} %reshape.17.rhs, f32[64,1536]{1,0:T(8,128)} %get-tuple-element.5.factor, f32[64,1536]{1,0:T(8,128)} %get-tuple-element.4.tissue, f32[64,1536]{1,0:T(8,128)} %copy.19.mean), custom_call_target="tpu_custom_call" | custom-call | tf_op jit(solution)/shard_map/solve/pallas_call | solution.py:148
  150.7 2.1 copy.20
  152.9 1.0 copy-done
  153.9 0.9 reshape.19
  154.7 20.3 %all-to-all-start.2 = ((f32[16,4,1536]{2,1,0:T(4,128)}), f32[16,4,1536]{2,1,0:T(4,128)S(1)}, u32[]{:S(2)}, u32[]{:S(2)}) async-start(f32[16,4,1536]{2,1,0:T(4,128)} %reshape.19), calls=%async_computation.2 | async-start | bytes 786432 | tf_op jit(solution)/shard_map/all_to_all | solution.py:180
  175.1 127.5 %reduce-scatter.4.cloned.1.call-done = f32[48,64]{1,0:T(8,128)} async-done(((f32[1536,64]{1,0:T(8,128)}), f32[48,64]{1,0:T(8,128)}) %reduce-scatter.4.cloned.1.call-update) | async-done | bytes 12304
  302.5 0.8 copy.21
  303.4 0.7 reshape.25
  304.1 30.9 %all-to-all-start.3 = ((f32[16,1,192]{2,1,0:T(1,128)}), f32[16,1,192]{2,1,0:T(1,128)S(1)}, u32[]{:S(2)}, u32[]{:S(2)}) async-start(f32[16,1,192]{2,1,0:T(1,128)} %reshape.25), calls=%async_computation.3 | async-start | bytes 32768 | tf_op jit(solution)/shard_map/all_to_all | solution.py:182
  334.9 9.7 %all-to-all-done.3 = f32[16,1,192]{2,1,0:T(1,128)S(1)} async-done(((f32[16,1,192]{2,1,0:T(1,128)}), f32[16,1,192]{2,1,0:T(1,128)S(1)}, u32[]{:S(2)}, u32[]{:S(2)}) %all-to-all-start.3) | async-done | bytes 12320 | tf_op jit(solution)/shard_map/all_to_all | solution.py:182
  344.6 0.6 reduce.1
  345.3 0.7 copy-done.1
  346.0 0.6 multiply_add_fusion
  346.6 0.7 copy.27
  (24 shorter events, 1.5 us)
Async XLA Ops:
  8.6 11.2 %copy-start.2 = (s32[4,1536]{1,0:T(4,128)S(1)}, s32[4,1536]{1,0:T(4,128)}, u32[]{:S(2)}) copy-start(s32[4,1536]{1,0:T(4,128)} %param.15) | copy-start | bytes 73732
  8.6 46.0 %all-to-all-start.1 = ((f32[16,1,192]{2,1,0:T(1,128)}), f32[16,1,192]{2,1,0:T(1,128)S(1)}, u32[]{:S(2)}, u32[]{:S(2)}) async-start(f32[16,1,192]{2,1,0:T(1,128)} %reshape.23), calls=%async_computation.1 | async-start | bytes 32768 | tf_op jit(solution)/shard_map/all_to_all | solution.py:177
  19.8 0.7 copy-start.5
  19.9 0.7 copy-start.3
  19.9 0.7 copy-start.4
  54.6 86.9 %all-to-all-start = ((f32[16,4,1536]{2,1,0:T(4,128)}), f32[16,4,1536]{2,1,0:T(4,128)S(1)}, u32[]{:S(2)}, u32[]{:S(2)}) async-start(f32[16,4,1536]{2,1,0:T(4,128)} %bitcast.2), calls=%async_computation | async-start | bytes 786432 | tf_op jit(solution)/shard_map/all_to_all | solution.py:176
  58.1 244.4 %reduce-scatter.4.cloned.1.call-start = ((), (), s32[]{:S(2)}) async-start(), calls=%async_computation.5 | async-start | bytes 811008
  152.9 1.0 copy-start
  154.7 149.3 %all-to-all-start.2 = ((f32[16,4,1536]{2,1,0:T(4,128)}), f32[16,4,1536]{2,1,0:T(4,128)S(1)}, u32[]{:S(2)}, u32[]{:S(2)}) async-start(f32[16,4,1536]{2,1,0:T(4,128)} %reshape.19), calls=%async_computation.2 | async-start | bytes 786432 | tf_op jit(solution)/shard_map/all_to_all | solution.py:180
  304.1 40.6 %all-to-all-start.3 = ((f32[16,1,192]{2,1,0:T(1,128)}), f32[16,1,192]{2,1,0:T(1,128)S(1)}, u32[]{:S(2)}, u32[]{:S(2)}) async-start(f32[16,1,192]{2,1,0:T(1,128)} %reshape.25), calls=%async_computation.3 | async-start | bytes 32768 | tf_op jit(solution)/shard_map/all_to_all | solution.py:182
  345.2 0.8 copy-start.1
Sparse Core Ops, SparseCore 0:
  153.0 149.4 reduce-scatter.3

commit v2 on v1

--- a/solution.py
+++ b/solution.py
@@ -49,9 +49,50 @@
     return jnp.sum(parts[0], axis=(0, 1), keepdims=True)
 
 
+def unpack_pieces(pieces, padded):
+    count, half, _ = pieces.shape
+    cells = padded.shape[1]
+    width = cells // count
+    lane = lax.broadcasted_iota(jnp.int32, (half, LANES), 1)
+    for upper in range(2):
+        for t in range(cells // LANES):
+            value = None
+            first = LANES * t // width
+            for piece in range(first, (LANES * (t + 1) - 1) // width + 1):
+                start = piece * width - LANES * t
+                moved = pieces[piece]
+                turn = (start - upper * width) % LANES
+                if turn:
+                    moved = pltpu.roll(moved, turn, 1)
+                value = moved if value is None else jnp.where(lane >= start, moved, value)
+            padded[8 + upper * half : 8 + (upper + 1) * half, LANES * t : LANES * (t + 1)] = value
+
+
+def pack_pieces(fields, pieces):
+    count, half, _ = pieces.shape
+    cells = fields.shape[1]
+    width = cells // count
+    lane = lax.broadcasted_iota(jnp.int32, (half, LANES), 1)
+    for piece in range(count):
+        t, offset = divmod(piece * width, LANES)
+        sides = []
+        for upper in range(2):
+            turn = (upper * width - offset) % LANES
+            value = None
+            for source in range(t, (piece * width + width - 1) // LANES + 1):
+                tile = fields[half * upper : half * (upper + 1), LANES * source : LANES * (source + 1)]
+                moved = pltpu.roll(tile, turn, 1) if turn else tile
+                if value is None:
+                    value = moved
+                else:
+                    value = jnp.where(lane < LANES - offset + upper * width, value, moved)
+            sides.append(value)
+        pieces[piece] = jnp.where(lane < width, sides[0], sides[1])
+
+
 def solve_kernel(
-    design, kappa, scale_ref, rhs, factor, tissue, mean, out, direction, padded_mean, residual,
-    applied, diagonal,
+    design, kappa, scale_ref, rhs, factor, tissue, mean, out, pieces, direction, padded_mean,
+    residual, applied, diagonal,
 ):
     regressor = lax.axis_index("slab")
     planes, cells = out.shape
@@ -63,7 +104,7 @@
     for ref in (direction, padded_mean):
         ref[0:8, :] = edge
         ref[8 + planes : 16 + planes, :] = edge
-    padded_mean[8 : 8 + planes, :] = mean[...]
+    unpack_pieces(mean, padded_mean)
     norms = []
     for block in range(blocks):
         center, sums = beside_tiles(padded_mean, block, columns)
@@ -128,6 +169,7 @@
                 out[at] += step_size * direction[8 + 8 * block : 16 + 8 * block, at[1]]
 
     last(lax.fori_loop(0, ITERS - 1, step, total(norms)))
+    pack_pieces(out, pieces)
 
 
 def total_tile(parts):
@@ -147,9 +189,12 @@
     padded = pltpu.VMEM((planes + 16, cells), jnp.float32)
     return pl.pallas_call(
         solve_kernel,
-        out_shape=jax.ShapeDtypeStruct((planes, cells), jnp.float32),
+        out_shape=[
+            jax.ShapeDtypeStruct((planes, cells), jnp.float32),
+            jax.ShapeDtypeStruct(mean.shape, jnp.float32),
+        ],
         in_specs=[smem] * 3 + [vmem] * 4,
-        out_specs=vmem,
+        out_specs=[vmem, vmem],
         scratch_shapes=[padded, padded, field, field, field],
         name="solve",
     )(design, kappa_sq, prior_scale, rhs, factor, tissue, mean)
@@ -167,20 +212,31 @@
     mean_field,
     pop_noise,
 ):
-    slabs = lax.axis_size("slab")
+    slabs, subjects = lax.axis_size("slab"), lax.axis_size("subj")
     depth, cells = tissue.shape
     planes = slabs * depth
+    width = cells // subjects
+    half = planes // 2
+
+    def exchange(values, axis):
+        return lax.all_to_all(values, axis, 0, 0, tiled=True)
+
+    def gather(values, axis):
+        return exchange(jnp.broadcast_to(values, (lax.axis_size(axis),) + values.shape), axis)
+
+    mean = exchange(mean_field, "slab").reshape(2, half, width)
+    spare = jnp.zeros((half, LANES - 2 * width), jnp.float32)
+    mean = gather(jnp.concatenate([mean[0], mean[1], spare], axis=1), "subj")
+    rhs = exchange(data_rhs[0], "slab").reshape(planes, cells)
     factor = inv_var[0] * (brain_mask.astype(jnp.float32) * keep_mask[0].astype(jnp.float32))
-    sent = jnp.stack([factor, tissue.astype(jnp.float32)])
-    both = lax.all_gather(sent, "slab", axis=1, tiled=True)
-    rhs = lax.all_to_all(data_rhs[0], "slab", 0, 0, tiled=True).reshape(planes, cells)
-    mean = lax.all_to_all(mean_field, "slab", 0, 0, tiled=True).reshape(planes, -1)
-    mean = lax.all_gather(mean, "subj", axis=1, tiled=True)
-    fields = solve(design, kappa_sq, prior_scale, rhs, both[0], both[1], mean)
-    back = lax.all_to_all(fields.reshape(slabs, depth, cells), "slab", 0, 0, tiled=True)
-    summed = lax.psum_scatter(fields, "subj", scatter_dimension=1, tiled=True)
-    summed = lax.all_to_all(summed.reshape(slabs, depth, -1), "slab", 0, 0, tiled=True)
-    divisor = lax.axis_size("subj") + MEAN_PRECISION
+    factor = gather(factor, "slab").reshape(planes, cells)
+    label = gather(tissue.astype(jnp.float32), "slab").reshape(planes, cells)
+    fields, pieces = solve(design, kappa_sq, prior_scale, rhs, factor, label, mean)
+    summed = jnp.sum(exchange(pieces, "subj"), axis=0)
+    summed = jnp.concatenate([summed[:, :width], summed[:, width : 2 * width]], axis=0)
+    summed = exchange(summed.reshape(slabs, depth, width), "slab")
+    back = exchange(fields.reshape(slabs, depth, cells), "slab")
+    divisor = subjects + MEAN_PRECISION
     new_mean = summed / divisor + pop_noise / math.sqrt(divisor)
     return (back[None], new_mean)
 

time: 355 us -> 183 us (0.52)
  blocking collectives: 113 us -> 20.6 us
  waiting for transfers between devices: 137 us -> 85.6 us
  starting transfers between devices: 65.9 us -> 51 us
  between operations: 14.1 us -> 0.75 us
    unnamed x2 -> x0, waiting for transfers between devices: 127 us -> none
    all_gather x2 -> x0, blocking collectives: 113 us -> none  [the longest x1 79.6 us: local(): mean = lax.all_gather(mean, 'subj', axis=1, tiled=True)]
    all_to_all x4 -> x7, waiting for transfers between devices: 9.71 us -> 85.6 us  [exchange(): return lax.all_to_all(values, axis, 0, 0, tiled=True)]
    all_to_all x0 -> x1, blocking collectives: none -> 20.6 us  [exchange(): return lax.all_to_all(values, axis, 0, 0, tiled=True)]
    all_to_all x4 -> x7, starting transfers between devices: 65.9 us -> 51 us  [exchange(): return lax.all_to_all(values, axis, 0, 0, tiled=True)]
    unnamed x19, local copies, waits for them, and re-layouts: 8.41 us -> 3.95 us
  transfers between devices with their start and end apart: 5 -> 7, of which waited for: 2 -> 7; matrix products, arithmetic and copies ran while one was open for 2% -> 3% of each run, Pallas kernels for 0% -> 0%
where the time goes in v2:
time: 183 us; the launch traced here: 180 us
  waiting for transfers between devices  85.6 us (47%)
  starting transfers between devices  51 us (28%)
  blocking collectives  20.6 us (11%)
  local copies, waits for them, and re-layouts  10.6 us (6%)
  Pallas kernels  9.05 us (5%)
  other arithmetic  2.11 us (1%)
    all_to_all x7, waiting for transfers between devices, exchange(): return lax.all_to_all(values, axis, 0, 0, tiled=True)  85.6 us
    all_to_all x7, starting transfers between devices, exchange(): return lax.all_to_all(values, axis, 0, 0, tiled=True)  51 us
    all_to_all x1, blocking collectives, exchange(): return lax.all_to_all(values, axis, 0, 0, tiled=True)  20.6 us
    pallas_call x1, Pallas kernels, solve(): pl.pallas_call(solve_kernel, out_shape=[jax.ShapeDtypeStruct((planes, cel...  9.05 us
    unnamed x19, local copies, waits for them, and re-layouts  3.95 us
  transfers between devices with their start and end apart: 7, of which 7 were waited for; matrix products, arithmetic and copies ran while one was open for 3% of the time, Pallas kernels for 0%

profile of v2, /device:TPU:1, one launch (start us, length us, event | category | flops | bytes accessed | tf_op | source)
XLA Modules:
  0.0 179.7 jit_solution(8091260010705918385)
XLA Ops:
  0.6 0.9 reshape.30
  1.5 20.6 %all_to_all.40 = f32[16,1,192]{2,1,0:T(1,128)S(1)} all-to-all(f32[16,1,192]{2,1,0:T(1,128)S(1)} %reshape.30), channel_id=1, replica_groups=mesh['subj'=32,'slab'=16] {'slab'}, dimensions={0} | all-to-all | bytes 24576 | tf_op jit(solution)/shard_map/all_to_all | solution.py:222
  22.1 3.9 %all-to-all-start = ((f32[16,4,1536]{2,1,0:T(4,128)}), f32[16,4,1536]{2,1,0:T(4,128)S(1)}, u32[]{:S(2)}, u32[]{:S(2)}) async-start(f32[16,4,1536]{2,1,0:T(4,128)} %bitcast.12), calls=%async_computation | async-start | bytes 786432 | tf_op jit(solution)/shard_map/all_to_all | solution.py:222
  25.9 14.3 %all-to-all-done = f32[16,4,1536]{2,1,0:T(4,128)S(1)} async-done(((f32[16,4,1536]{2,1,0:T(4,128)}), f32[16,4,1536]{2,1,0:T(4,128)S(1)}, u32[]{:S(2)}, u32[]{:S(2)}) %all-to-all-start) | async-done | bytes 393248 | tf_op jit(solution)/shard_map/all_to_all | solution.py:222
  40.2 0.8 broadcast_in_dim.16
  41.0 4.7 %all-to-all-start.2 = ((f32[16,4,1536]{2,1,0:T(4,128)}), f32[16,4,1536]{2,1,0:T(4,128)S(1)}, u32[]{:S(2)}, u32[]{:S(2)}) async-start(f32[16,4,1536]{2,1,0:T(4,128)} %broadcast_in_dim.16), calls=%async_computation.2 | async-start | bytes 786432 | tf_op jit(solution)/shard_map/all_to_all | solution.py:222
  45.7 12.3 %all-to-all-done.2 = f32[16,4,1536]{2,1,0:T(4,128)S(1)} async-done(((f32[16,4,1536]{2,1,0:T(4,128)}), f32[16,4,1536]{2,1,0:T(4,128)S(1)}, u32[]{:S(2)}, u32[]{:S(2)}) %all-to-all-start.2) | async-done | bytes 393248 | tf_op jit(solution)/shard_map/all_to_all | solution.py:222
  58.1 0.8 broadcast_in_dim.15
  58.9 6.6 %all-to-all-start.1 = ((f32[16,4,1536]{2,1,0:T(4,128)}), f32[16,4,1536]{2,1,0:T(4,128)S(1)}, u32[]{:S(2)}, u32[]{:S(2)}) async-start(f32[16,4,1536]{2,1,0:T(4,128)} %broadcast_in_dim.15), calls=%async_computation.1 | async-start | bytes 786432 | tf_op jit(solution)/shard_map/all_to_all | solution.py:222
  67.0 10.8 %all-to-all-done.1 = f32[16,4,1536]{2,1,0:T(4,128)S(1)} async-done(((f32[16,4,1536]{2,1,0:T(4,128)}), f32[16,4,1536]{2,1,0:T(4,128)S(1)}, u32[]{:S(2)}, u32[]{:S(2)}) %all-to-all-start.1) | async-done | bytes 393248 | tf_op jit(solution)/shard_map/all_to_all | solution.py:222
  77.8 0.8 broadcast_in_dim.18
  78.6 17.1 %all-to-all-start.4 = ((f32[32,32,128]{2,1,0:T(8,128)}), f32[32,32,128]{2,1,0:T(8,128)S(1)}, u32[]{:S(2)}, u32[]{:S(2)}) async-start(f32[32,32,128]{2,1,0:T(8,128)} %broadcast_in_dim.18), calls=%async_computation.4 | async-start | bytes 1048576 | tf_op jit(solution)/shard_map/all_to_all | solution.py:222
  95.7 0.9 reshape.25.rhs
  96.6 0.9 reshape.27.tissue
  97.5 0.9 reshape.26.factor
  98.4 12.6 %all-to-all-done.4.mean = f32[32,32,128]{2,1,0:T(8,128)S(1)} async-done(((f32[32,32,128]{2,1,0:T(8,128)}), f32[32,32,128]{2,1,0:T(8,128)S(1)}, u32[]{:S(2)}, u32[]{:S(2)}) %all-to-all-start.4) | async-done | bytes 524320 | tf_op jit(solution)/shard_map/all_to_all | solution.py:222
  111.8 9.0 %solve.1 = (f32[64,1536]{1,0:T(8,128)}, f32[32,32,128]{2,1,0:T(8,128)}) custom-call(f32[1,16]{1,0:T(1,128)} %design.1, f32[3,16]{1,0:T(4,128)} %kappa.1, f32[16]{0:T(128)} %scale_ref.1, f32[64,1536]{1,0:T(8,128)} %reshape.25.rhs, f32[64,1536]{1,0:T(8,128)} %reshape.26.factor, f32[64,1536]{1,0:T(8,128)} %reshape.27.tissue, f32[32,32,128]{2,1,0:T(8,128)} %copy-done), custom_call_target="tpu_custom_call" | custom-call | tf_op jit(solution)/shard_map/solve/pallas_call | solution.py:190
  120.8 6.6 %all-to-all-start.6 = ((f32[32,32,128]{2,1,0:T(8,128)}), f32[32,32,128]{2,1,0:T(8,128)S(1)}, u32[]{:S(2)}, u32[]{:S(2)}) async-start(f32[32,32,128]{2,1,0:T(8,128)} %get-tuple-element.5), calls=%async_computation.6 | async-start | bytes 1048576 | tf_op jit(solution)/shard_map/all_to_all | solution.py:222
  127.5 0.9 reshape.28
  128.4 14.3 %all-to-all-done.6 = f32[32,32,128]{2,1,0:T(8,128)S(1)} async-done(((f32[32,32,128]{2,1,0:T(8,128)}), f32[32,32,128]{2,1,0:T(8,128)S(1)}, u32[]{:S(2)}, u32[]{:S(2)}) %all-to-all-start.6) | async-done | bytes 524320 | tf_op jit(solution)/shard_map/all_to_all | solution.py:222
  142.7 6.3 %all-to-all-start.5 = ((f32[16,4,1536]{2,1,0:T(4,128)}), f32[16,4,1536]{2,1,0:T(4,128)S(1)}, u32[]{:S(2)}, u32[]{:S(2)}) async-start(f32[16,4,1536]{2,1,0:T(4,128)} %reshape.28), calls=%async_computation.5 | async-start | bytes 786432 | tf_op jit(solution)/shard_map/all_to_all | solution.py:222
  149.8 11.6 %all-to-all-done.5 = f32[16,4,1536]{2,1,0:T(4,128)S(1)} async-done(((f32[16,4,1536]{2,1,0:T(4,128)}), f32[16,4,1536]{2,1,0:T(4,128)S(1)}, u32[]{:S(2)}, u32[]{:S(2)}) %all-to-all-start.5) | async-done | bytes 393248 | tf_op jit(solution)/shard_map/all_to_all | solution.py:222
  161.5 5.7 %all-to-all-start.7 = ((f32[16,1,192]{2,1,0:T(1,128)}), f32[16,1,192]{2,1,0:T(1,128)S(1)}, u32[]{:S(2)}, u32[]{:S(2)}) async-start(f32[16,1,192]{2,1,0:T(1,128)} %reshape.32), calls=%async_computation.7 | async-start | bytes 32768 | tf_op jit(solution)/shard_map/all_to_all | solution.py:222
  167.2 9.7 %all-to-all-done.7 = f32[16,1,192]{2,1,0:T(1,128)S(1)} async-done(((f32[16,1,192]{2,1,0:T(1,128)}), f32[16,1,192]{2,1,0:T(1,128)S(1)}, u32[]{:S(2)}, u32[]{:S(2)}) %all-to-all-start.7) | async-done | bytes 12320 | tf_op jit(solution)/shard_map/all_to_all | solution.py:222
  (31 shorter events, 5.9 us)
Async XLA Ops:
  22.1 3.9 %copy-start.3 = (s32[4,1536]{1,0:T(4,128)S(1)}, s32[4,1536]{1,0:T(4,128)}, u32[]{:S(2)}) copy-start(s32[4,1536]{1,0:T(4,128)} %param.15) | copy-start | bytes 73732
  22.1 18.2 %all-to-all-start = ((f32[16,4,1536]{2,1,0:T(4,128)}), f32[16,4,1536]{2,1,0:T(4,128)S(1)}, u32[]{:S(2)}, u32[]{:S(2)}) async-start(f32[16,4,1536]{2,1,0:T(4,128)} %bitcast.12), calls=%async_computation | async-start | bytes 786432 | tf_op jit(solution)/shard_map/all_to_all | solution.py:222
  41.0 4.7 %copy-start.4 = (f32[1,4,1536]{2,1,0:T(4,128)S(1)}, f32[1,4,1536]{2,1,0:T(4,128)}, u32[]{:S(2)}) copy-start(f32[1,4,1536]{2,1,0:T(4,128)} %param.11) | copy-start | bytes 73732
  41.0 4.7 %copy-start.5 = (s32[1,4,1536]{2,1,0:T(4,128)S(1)}, s32[1,4,1536]{2,1,0:T(4,128)}, u32[]{:S(2)}) copy-start(s32[1,4,1536]{2,1,0:T(4,128)} %param.13) | copy-start | bytes 73732
  41.0 4.7 %copy-start.6 = (s32[4,1536]{1,0:T(4,128)S(1)}, s32[4,1536]{1,0:T(4,128)}, u32[]{:S(2)}) copy-start(s32[4,1536]{1,0:T(4,128)} %param.14) | copy-start | bytes 73732
  41.0 17.0 %all-to-all-start.2 = ((f32[16,4,1536]{2,1,0:T(4,128)}), f32[16,4,1536]{2,1,0:T(4,128)S(1)}, u32[]{:S(2)}, u32[]{:S(2)}) async-start(f32[16,4,1536]{2,1,0:T(4,128)} %broadcast_in_dim.16), calls=%async_computation.2 | async-start | bytes 786432 | tf_op jit(solution)/shard_map/all_to_all | solution.py:222
  58.9 18.9 %all-to-all-start.1 = ((f32[16,4,1536]{2,1,0:T(4,128)}), f32[16,4,1536]{2,1,0:T(4,128)S(1)}, u32[]{:S(2)}, u32[]{:S(2)}) async-start(f32[16,4,1536]{2,1,0:T(4,128)} %broadcast_in_dim.15), calls=%async_computation.1 | async-start | bytes 786432 | tf_op jit(solution)/shard_map/all_to_all | solution.py:222
  78.6 32.4 %all-to-all-start.4 = ((f32[32,32,128]{2,1,0:T(8,128)}), f32[32,32,128]{2,1,0:T(8,128)S(1)}, u32[]{:S(2)}, u32[]{:S(2)}) async-start(f32[32,32,128]{2,1,0:T(8,128)} %broadcast_in_dim.18), calls=%async_computation.4 | async-start | bytes 1048576 | tf_op jit(solution)/shard_map/all_to_all | solution.py:222
  111.0 0.8 copy-start
  120.8 6.7 %copy-start.1 = (f32[64,1536]{1,0:T(8,128)S(1)}, f32[64,1536]{1,0:T(8,128)}, u32[]{:S(2)}) copy-start(f32[64,1536]{1,0:T(8,128)} %get-tuple-element.4) | copy-start | bytes 1179652
  120.8 21.8 %all-to-all-start.6 = ((f32[32,32,128]{2,1,0:T(8,128)}), f32[32,32,128]{2,1,0:T(8,128)S(1)}, u32[]{:S(2)}, u32[]{:S(2)}) async-start(f32[32,32,128]{2,1,0:T(8,128)} %get-tuple-element.5), calls=%async_computation.6 | async-start | bytes 1048576 | tf_op jit(solution)/shard_map/all_to_all | solution.py:222
  142.7 18.8 %all-to-all-start.5 = ((f32[16,4,1536]{2,1,0:T(4,128)}), f32[16,4,1536]{2,1,0:T(4,128)S(1)}, u32[]{:S(2)}, u32[]{:S(2)}) async-start(f32[16,4,1536]{2,1,0:T(4,128)} %reshape.28), calls=%async_computation.5 | async-start | bytes 786432 | tf_op jit(solution)/shard_map/all_to_all | solution.py:222
  161.5 15.4 %all-to-all-start.7 = ((f32[16,1,192]{2,1,0:T(1,128)}), f32[16,1,192]{2,1,0:T(1,128)S(1)}, u32[]{:S(2)}, u32[]{:S(2)}) async-start(f32[16,1,192]{2,1,0:T(1,128)} %reshape.32), calls=%async_computation.7 | async-start | bytes 32768 | tf_op jit(solution)/shard_map/all_to_all | solution.py:222
  177.6 0.8 copy-start.2

commit v3 on v2

--- a/solution.py
+++ b/solution.py
@@ -65,14 +65,20 @@
                 if turn:
                     moved = pltpu.roll(moved, turn, 1)
                 value = moved if value is None else jnp.where(lane >= start, moved, value)
-            padded[8 + upper * half : 8 + (upper + 1) * half, LANES * t : LANES * (t + 1)] = value
-
-
-def pack_pieces(fields, pieces):
+            for pair in range(half // 2):
+                row = 8 + 4 * pair + 2 * upper
+                padded[row : row + 2, LANES * t : LANES * (t + 1)] = value[2 * pair : 2 * pair + 2]
+
+
+def pack_pieces(fields, pieces, halves):
     count, half, _ = pieces.shape
     cells = fields.shape[1]
     width = cells // count
     lane = lax.broadcasted_iota(jnp.int32, (half, LANES), 1)
+    for upper in range(2):
+        for pair in range(half // 2):
+            row = 4 * pair + 2 * upper
+            halves[upper, 2 * pair : 2 * pair + 2, :] = fields[row : row + 2, :]
     for piece in range(count):
         t, offset = divmod(piece * width, LANES)
         sides = []
@@ -80,7 +86,7 @@
             turn = (upper * width - offset) % LANES
             value = None
             for source in range(t, (piece * width + width - 1) // LANES + 1):
-                tile = fields[half * upper : half * (upper + 1), LANES * source : LANES * (source + 1)]
+                tile = halves[upper, :, LANES * source : LANES * (source + 1)]
                 moved = pltpu.roll(tile, turn, 1) if turn else tile
                 if value is None:
                     value = moved
@@ -91,8 +97,8 @@
 
 
 def solve_kernel(
-    design, kappa, scale_ref, rhs, factor, tissue, mean, out, pieces, direction, padded_mean,
-    residual, applied, diagonal,
+    design, kappa, scale_ref, rhs, both, mean, slab_fields, pieces, direction, padded_mean, residual,
+    applied, diagonal, out, halves,
 ):
     regressor = lax.axis_index("slab")
     planes, cells = out.shape
@@ -105,20 +111,26 @@
         ref[0:8, :] = edge
         ref[8 + planes : 16 + planes, :] = edge
     unpack_pieces(mean, padded_mean)
+    depth = planes // rhs.shape[0]
+    for slab in range(rhs.shape[0]):
+        rows = slice(depth * slab, depth * (slab + 1))
+        residual[rows, :] = rhs[slab]
+        diagonal[rows, :] = both[slab, 0]
+        applied[rows, :] = both[slab, 1]
     norms = []
     for block in range(blocks):
         center, sums = beside_tiles(padded_mean, block, columns)
         for t in range(columns):
             at = (slice(8 * block, 8 * block + 8), slice(LANES * t, LANES * (t + 1)))
-            label = tissue[at]
+            label = applied[at]
             kappa_field = jnp.where(
                 label == 0,
                 kappa[0, regressor],
                 jnp.where(label == 1, kappa[1, regressor], kappa[2, regressor]),
             )
             shifted = 6.0 + kappa_field
-            right_side = rhs[at] + scale * (shifted * center[t] - sums[t])
-            diagonal[at] = design_k * factor[at] + scale * shifted
+            right_side = residual[at] + scale * (shifted * center[t] - sums[t])
+            diagonal[at] = design_k * diagonal[at] + scale * shifted
             residual[at] = right_side
             direction[8 + 8 * block : 16 + 8 * block, at[1]] = right_side
             norms.append(right_side * right_side)
@@ -169,7 +181,9 @@
                 out[at] += step_size * direction[8 + 8 * block : 16 + 8 * block, at[1]]
 
     last(lax.fori_loop(0, ITERS - 1, step, total(norms)))
-    pack_pieces(out, pieces)
+    for slab in range(rhs.shape[0]):
+        slab_fields[slab] = out[depth * slab : depth * (slab + 1), :]
+    pack_pieces(out, pieces, halves)
 
 
 def total_tile(parts):
@@ -181,23 +195,172 @@
     return parts[0]
 
 
-def solve(design, kappa_sq, prior_scale, rhs, factor, tissue, mean):
-    planes, cells = rhs.shape
+def solve(design, kappa_sq, prior_scale, rhs, both, mean):
+    slabs, depth, cells = rhs.shape
+    planes = slabs * depth
     vmem = pl.BlockSpec(memory_space=pltpu.VMEM)
     smem = pl.BlockSpec(memory_space=pltpu.SMEM)
     field = pltpu.VMEM((planes, cells), jnp.float32)
     padded = pltpu.VMEM((planes + 16, cells), jnp.float32)
+    halves = pltpu.VMEM((2, planes // 2, cells), jnp.float32)
     return pl.pallas_call(
         solve_kernel,
         out_shape=[
-            jax.ShapeDtypeStruct((planes, cells), jnp.float32),
+            jax.ShapeDtypeStruct(rhs.shape, jnp.float32),
             jax.ShapeDtypeStruct(mean.shape, jnp.float32),
         ],
-        in_specs=[smem] * 3 + [vmem] * 4,
+        in_specs=[smem] * 3 + [vmem] * 3,
         out_specs=[vmem, vmem],
-        scratch_shapes=[padded, padded, field, field, field],
+        scratch_shapes=[padded, padded, field, field, field, field, halves],
         name="solve",
-    )(design, kappa_sq, prior_scale, rhs, factor, tissue, mean)
+    )(design, kappa_sq, prior_scale, rhs, both, mean)
+
+
+def greet(axes):
+    barrier = pltpu.get_barrier_semaphore()
+    peers = 0
+    for axis in axes:
+        size, me = lax.axis_size(axis), lax.axis_index(axis)
+
+        def signal(offset, carry):
+            pl.semaphore_signal(
+                barrier,
+                inc=1,
+                device_id={axis: lax.rem(me + offset, size)},
+                device_id_type=pl.DeviceIdType.MESH,
+            )
+            return carry
+
+        lax.fori_loop(1, size, signal, 0)
+        peers += size - 1
+    pl.semaphore_wait(barrier, peers)
+
+
+class Exchange:
+    def __init__(self, source, target, axis, sems, whole=False):
+        self.size, self.me = lax.axis_size(axis), lax.axis_index(axis)
+        self.source, self.target, self.axis, self.whole = source, target, axis, whole
+        self.send, self.receive, self.own = sems
+
+    def block(self, index):
+        return self.source if self.whole else self.source.at[index]
+
+    def remote(self, offset):
+        to = lax.rem(self.me + offset, self.size)
+        return pltpu.make_async_remote_copy(
+            src_ref=self.block(to),
+            dst_ref=self.target.at[self.me],
+            send_sem=self.send.at[offset - 1],
+            recv_sem=self.receive.at[offset - 1],
+            device_id={self.axis: to},
+            device_id_type=pl.DeviceIdType.MESH,
+        )
+
+    def local(self):
+        return pltpu.make_async_copy(self.block(self.me), self.target.at[self.me], self.own)
+
+    def start(self):
+        def one(offset, carry):
+            self.remote(offset).start()
+            return carry
+
+        lax.fori_loop(1, self.size, one, 0)
+        self.local().start()
+
+    def wait(self):
+        def one(offset, carry):
+            self.remote(offset).wait()
+            return carry
+
+        self.local().wait()
+        lax.fori_loop(1, self.size, one, 0)
+
+
+def exchange_sems(axis):
+    count = lax.axis_size(axis) - 1
+    return [
+        pltpu.SemaphoreType.DMA((count,)),
+        pltpu.SemaphoreType.DMA((count,)),
+        pltpu.SemaphoreType.DMA,
+    ]
+
+
+def bring_kernel(rhs, both, mean, rhs_out, both_out, mean_out, held, *sems):
+    small = Exchange(mean, held, "slab", sems[0:3])
+    spread = Exchange(held, mean_out, "subj", sems[3:6], whole=True)
+    large = Exchange(rhs, rhs_out, "slab", sems[6:9])
+    shared = Exchange(both, both_out, "slab", sems[9:12], whole=True)
+    greet(("slab", "subj"))
+    small.start()
+    large.start()
+    shared.start()
+    small.wait()
+    spread.start()
+    large.wait()
+    shared.wait()
+    spread.wait()
+
+
+def bring(rhs, both, mean):
+    slabs, subjects = lax.axis_size("slab"), lax.axis_size("subj")
+    vmem = pl.BlockSpec(memory_space=pltpu.VMEM)
+    return pl.pallas_call(
+        bring_kernel,
+        out_shape=[
+            jax.ShapeDtypeStruct(rhs.shape, jnp.float32),
+            jax.ShapeDtypeStruct((slabs,) + both.shape, jnp.float32),
+            jax.ShapeDtypeStruct((subjects,) + mean.shape, jnp.float32),
+        ],
+        in_specs=[vmem] * 3,
+        out_specs=[vmem] * 3,
+        scratch_shapes=[
+            pltpu.VMEM(mean.shape, jnp.float32),
+            *exchange_sems("slab"),
+            *exchange_sems("subj"),
+            *exchange_sems("slab"),
+            *exchange_sems("slab"),
+        ],
+        compiler_params=pltpu.CompilerParams(collective_id=0, has_side_effects=True),
+        name="bring",
+    )(rhs, both, mean)
+
+
+def give_kernel(fields, pieces, fields_out, mean_out, arrived, summed, *sems):
+    parts = Exchange(pieces, arrived, "subj", sems[0:3])
+    large = Exchange(fields, fields_out, "slab", sems[3:6])
+    small = Exchange(summed, mean_out, "slab", sems[6:9])
+    greet(("slab", "subj"))
+    parts.start()
+    large.start()
+    parts.wait()
+    summed[...] = jnp.sum(arrived[...], axis=0)
+    small.start()
+    large.wait()
+    small.wait()
+
+
+def give(fields, pieces):
+    slabs = lax.axis_size("slab")
+    vmem = pl.BlockSpec(memory_space=pltpu.VMEM)
+    small = (slabs,) + pieces.shape[2:]
+    return pl.pallas_call(
+        give_kernel,
+        out_shape=[
+            jax.ShapeDtypeStruct(fields.shape, jnp.float32),
+            jax.ShapeDtypeStruct(small, jnp.float32),
+        ],
+        in_specs=[vmem] * 2,
+        out_specs=[vmem] * 2,
+        scratch_shapes=[
+            pltpu.VMEM(pieces.shape, jnp.float32),
+            pltpu.VMEM(small, jnp.float32),
+            *exchange_sems("subj"),
+            *exchange_sems("slab"),
+            *exchange_sems("slab"),
+        ],
+        compiler_params=pltpu.CompilerParams(collective_id=1, has_side_effects=True),
+        name="give",
+    )(fields, pieces)
 
 
 def local(
@@ -214,28 +377,17 @@
 ):
     slabs, subjects = lax.axis_size("slab"), lax.axis_size("subj")
     depth, cells = tissue.shape
-    planes = slabs * depth
     width = cells // subjects
-    half = planes // 2
-
-    def exchange(values, axis):
-        return lax.all_to_all(values, axis, 0, 0, tiled=True)
-
-    def gather(values, axis):
-        return exchange(jnp.broadcast_to(values, (lax.axis_size(axis),) + values.shape), axis)
-
-    mean = exchange(mean_field, "slab").reshape(2, half, width)
-    spare = jnp.zeros((half, LANES - 2 * width), jnp.float32)
-    mean = gather(jnp.concatenate([mean[0], mean[1], spare], axis=1), "subj")
-    rhs = exchange(data_rhs[0], "slab").reshape(planes, cells)
+    pair = depth // 2
+    spare = jnp.zeros((slabs, pair, LANES - 2 * width), jnp.float32)
+    mean = jnp.concatenate([mean_field[:, :pair], mean_field[:, pair:], spare], axis=2)
     factor = inv_var[0] * (brain_mask.astype(jnp.float32) * keep_mask[0].astype(jnp.float32))
-    factor = gather(factor, "slab").reshape(planes, cells)
-    label = gather(tissue.astype(jnp.float32), "slab").reshape(planes, cells)
-    fields, pieces = solve(design, kappa_sq, prior_scale, rhs, factor, label, mean)
-    summed = jnp.sum(exchange(pieces, "subj"), axis=0)
-    summed = jnp.concatenate([summed[:, :width], summed[:, width : 2 * width]], axis=0)
-    summed = exchange(summed.reshape(slabs, depth, width), "slab")
-    back = exchange(fields.reshape(slabs, depth, cells), "slab")
+    both = jnp.stack([factor, tissue.astype(jnp.float32)])
+    rhs, both, mean = bring(data_rhs[0], both, mean)
+    mean = mean.reshape(subjects, slabs * pair, LANES)
+    fields, pieces = solve(design, kappa_sq, prior_scale, rhs, both, mean)
+    back, summed = give(fields, pieces.reshape(subjects, slabs, pair, LANES))
+    summed = jnp.concatenate([summed[..., :width], summed[..., width : 2 * width]], axis=1)
     divisor = subjects + MEAN_PRECISION
     new_mean = summed / divisor + pop_noise / math.sqrt(divisor)
     return (back[None], new_mean)

time: 183 us -> 113 us (0.62); the launches traced: 180 us -> 112 us
  Pallas kernels: 9.05 us -> 106 us
  waiting for transfers between devices: 85.6 us -> 0 us
  starting transfers between devices: 51 us -> 0 us
  blocking collectives: 20.6 us -> 0 us
  local copies, waits for them, and re-layouts: 10.6 us -> 2.86 us
    pallas_call x1 -> x3, Pallas kernels: 9.05 us -> 106 us  [the longest x1 57.7 us: bring(): pl.pallas_call(bring_kernel, out_shape=[jax.ShapeDtypeStruct(rhs.shape, j...]
    all_to_all x7 -> x0, waiting for transfers between devices: 85.6 us -> none  [exchange(): return lax.all_to_all(values, axis, 0, 0, tiled=True)]
    all_to_all x7 -> x0, starting transfers between devices: 51 us -> none  [exchange(): return lax.all_to_all(values, axis, 0, 0, tiled=True)]
    all_to_all x1 -> x0, blocking collectives: 20.6 us -> none  [exchange(): return lax.all_to_all(values, axis, 0, 0, tiled=True)]
    reshape x4 -> x0, local copies, waits for them, and re-layouts: 3.52 us -> none  [the longest x1 0.89 us: local(): label = gather(tissue.astype(jnp.float32), 'slab').reshape(planes, cells)]
    broadcast_in_dim x4 -> x1, local copies, waits for them, and re-layouts: 2.44 us -> 0.01 us  [local(): spare = jnp.zeros((slabs, pair, LANES - 2 * width), jnp.float32)]
    unnamed x19 -> x7, local copies, waits for them, and re-layouts: 3.95 us -> 1.9 us
  transfers between devices with their start and end apart: 7 -> 0, of which waited for: 7 -> 0; matrix products, arithmetic and copies ran while one was open for 3% -> 0% of each run, Pallas kernels for 0% -> 0%
where the time goes in v3:
time: 113 us; the launch traced here: 112 us
  Pallas kernels  106 us (94%)
  local copies, waits for them, and re-layouts  2.86 us (3%)
  other arithmetic  2.77 us (2%)
    pallas_call x1, Pallas kernels, bring(): pl.pallas_call(bring_kernel, out_shape=[jax.ShapeDtypeStruct(rhs.shape, j...  57.7 us
    pallas_call x1, Pallas kernels, give(): pl.pallas_call(give_kernel, out_shape=[jax.ShapeDtypeStruct(fields.shape,...  39 us
    pallas_call x1, Pallas kernels, solve(): pl.pallas_call(solve_kernel, out_shape=[jax.ShapeDtypeStruct(rhs.shape, j...  9.22 us

profile of v3, /device:TPU:1, one launch (start us, length us, event | category | flops | bytes accessed | tf_op | source)
XLA Modules:
  0.0 112.2 jit_solution(16511800677392045224)
XLA Ops:
  0.6 0.1 pad.4.clone
  0.7 0.0 copy-start.2
  0.7 0.8 fusion.2
  1.5 0.0 copy-done.2
  1.5 0.0 copy-start.1
  1.5 0.6 pad_maximum_fusion.both
  2.2 0.1 copy-done.1
  2.3 0.7 maximum_maximum_fusion.mean
  3.0 57.7 %bring.1 = (f32[16,4,1536]{2,1,0:T(4,128)}, f32[16,2,4,1536]{3,2,1,0:T(4,128)}, f32[32,16,2,128]{3,2,1,0:T(2,128)}) custom-call(f32[16,4,1536]{2,1,0:T(4,128)} %bitcast.18, f32[2,4,1536]{2,1,0:T(4,128)} %pad_maximum_fusion.both, f32[16,2,128]{2,1,0:T(2,128)} %maximum_maximum_fusion.mean), custom_call_target="tpu_custom_call" | custom-call | tf_op jit(solution)/shard_map/bring/pallas_call | solution.py:307
  60.7 9.2 %solve.1 = (f32[16,4,1536]{2,1,0:T(4,128)}, f32[32,32,128]{2,1,0:T(8,128)}) custom-call(f32[1,16]{1,0:T(1,128)} %design.1, f32[3,16]{1,0:T(4,128)} %kappa.1, f32[16]{0:T(128)} %scale_ref.1, f32[16,4,1536]{2,1,0:T(4,128)} %get-tuple-element.9.rhs, f32[16,2,4,1536]{3,2,1,0:T(4,128)} %get-tuple-element.10.both, f32[32,32,128]{2,1,0:T(8,128)} %bitcast.17), custom_call_target="tpu_custom_call" | custom-call | tf_op jit(solution)/shard_map/solve/pallas_call | solution.py:206
  70.0 39.0 %give.1 = (f32[16,4,1536]{2,1,0:T(4,128)}, f32[16,2,128]{2,1,0:T(2,128)}) custom-call(f32[16,4,1536]{2,1,0:T(4,128)} %get-tuple-element.12.fields, f32[32,16,2,128]{3,2,1,0:T(2,128)} %bitcast.16), custom_call_target="tpu_custom_call" | custom-call | tf_op jit(solution)/shard_map/give/pallas_call | solution.py:346
  108.9 0.0 copy-start
  108.9 0.9 fusion.4
  109.8 0.0 copy-done
  109.8 0.6 fusion
  110.5 1.8 %copy.13 = f32[1,16,4,1536]{3,2,1,0:T(4,128)} copy(f32[1,16,4,1536]{3,2,1,0:T(4,128)} %bitcast.19) | data formatting | bytes 786432
  (3 shorter events, 0.0 us)
Async XLA Ops:
  0.7 0.8 copy-start.2
  1.5 0.8 copy-start.1
  108.9 0.9 copy-start

commit v4 on v3

--- a/solution.py
+++ b/solution.py
@@ -11,6 +11,8 @@
 CX = 64
 LANES = 128
 MEAN_PRECISION = 1.0
+CORES = 2
+ROW = 4
 
 
 def tiles_of(ref, row, columns):
@@ -216,93 +218,154 @@
     )(design, kappa_sq, prior_scale, rhs, both, mean)
 
 
-def greet(axes):
+def ring(axis, stride, count):
+    index = lax.axis_index(axis)
+    place = lax.rem(lax.div(index, stride), count)
+    return axis, count - 1, lambda i: index + (lax.rem(place + i + 1, count) - place) * stride
+
+
+def across(axis, low):
+    index = lax.axis_index(axis)
+    place = lax.rem(index, low)
+    base = index - place
+    other = lax.rem(base + low, 2 * low)
+    return axis, low, lambda i: other + lax.rem(place + i, low)
+
+
+def greet(*groups):
     barrier = pltpu.get_barrier_semaphore()
-    peers = 0
-    for axis in axes:
-        size, me = lax.axis_size(axis), lax.axis_index(axis)
-
-        def signal(offset, carry):
+    for axis, count, peer in groups:
+
+        def signal(i, carry):
             pl.semaphore_signal(
-                barrier,
-                inc=1,
-                device_id={axis: lax.rem(me + offset, size)},
-                device_id_type=pl.DeviceIdType.MESH,
+                barrier, inc=1, device_id={axis: peer(i)}, device_id_type=pl.DeviceIdType.MESH
             )
             return carry
 
-        lax.fori_loop(1, size, signal, 0)
-        peers += size - 1
-    pl.semaphore_wait(barrier, peers)
+        lax.fori_loop(0, count, signal, 0)
+    pl.semaphore_wait(barrier, sum(count for _, count, _ in groups))
 
 
 class Exchange:
-    def __init__(self, source, target, axis, sems, whole=False):
-        self.size, self.me = lax.axis_size(axis), lax.axis_index(axis)
-        self.source, self.target, self.axis, self.whole = source, target, axis, whole
-        self.send, self.receive, self.own = sems
-
-    def block(self, index):
-        return self.source if self.whole else self.source.at[index]
-
-    def remote(self, offset):
-        to = lax.rem(self.me + offset, self.size)
+    def __init__(self, group, source, target, sems):
+        self.axis, self.count, self.peer = group
+        self.source, self.target = source, target
+        self.send, self.receive = sems
+
+    def remote(self, i):
+        to = self.peer(i)
         return pltpu.make_async_remote_copy(
-            src_ref=self.block(to),
-            dst_ref=self.target.at[self.me],
-            send_sem=self.send.at[offset - 1],
-            recv_sem=self.receive.at[offset - 1],
+            src_ref=self.source(i, to),
+            dst_ref=self.target(i),
+            send_sem=self.send.at[i],
+            recv_sem=self.receive.at[i],
             device_id={self.axis: to},
             device_id_type=pl.DeviceIdType.MESH,
         )
 
-    def local(self):
-        return pltpu.make_async_copy(self.block(self.me), self.target.at[self.me], self.own)
-
     def start(self):
-        def one(offset, carry):
-            self.remote(offset).start()
+        def one(i, carry):
+            self.remote(i).start()
             return carry
 
-        lax.fori_loop(1, self.size, one, 0)
-        self.local().start()
+        lax.fori_loop(0, self.count, one, 0)
 
     def wait(self):
-        def one(offset, carry):
-            self.remote(offset).wait()
+        def one(i, carry):
+            self.remote(i).wait()
             return carry
 
-        self.local().wait()
-        lax.fori_loop(1, self.size, one, 0)
-
-
-def exchange_sems(axis):
-    count = lax.axis_size(axis) - 1
-    return [
-        pltpu.SemaphoreType.DMA((count,)),
-        pltpu.SemaphoreType.DMA((count,)),
-        pltpu.SemaphoreType.DMA,
+        lax.fori_loop(0, self.count, one, 0)
+
+
+def exchange_sems(*counts):
+    return [pltpu.SemaphoreType.DMA((count,)) for count in counts for _ in range(2)]
+
+
+def bring_kernel(rhs, both, mean, rhs_out, both_out, mean_out, held, own, *sems):
+    slabs, subjects = rhs.shape[0], mean_out.shape[0]
+    slab, subject = lax.axis_index("slab"), lax.axis_index("subj")
+    half = slabs // 2
+    mirror = lax.rem(slab + half, slabs)
+    core = lax.rem(slab, CORES)
+    layer = pl.ds(subject - lax.rem(subject, ROW), ROW)
+    near = ring("slab", 1, half)
+    far = across("slab", half)
+    along_x = ring("slab", CORES, half // CORES)
+    along_y = ring("subj", 1, ROW)
+    along_z = ring("subj", ROW, subjects // ROW)
+    partner = ring("slab", 1, CORES)[2](0)
+
+    def pair(k):
+        return sems[2 * k], sems[2 * k + 1]
+
+    def take(ref):
+        return lambda i, to: ref.at[to]
+
+    def put(ref, index):
+        return lambda i: ref.at[index]
+
+    small_near = Exchange(near, take(mean), put(held, slab), pair(0))
+    small_far = Exchange(far, take(mean), put(held, slab), pair(1))
+    large_near = Exchange(near, take(rhs), put(rhs_out, slab), pair(2))
+    large_far = Exchange(far, take(rhs), put(rhs_out, slab), pair(3))
+    over = Exchange(
+        ("slab", 1, lambda i: mirror), lambda i, to: both, put(both_out, slab), pair(4)
+    )
+    beside = Exchange(along_x, lambda i, to: both, put(both_out, slab), pair(5))
+    passed = Exchange(
+        along_x, lambda i, to: both_out.at[mirror], put(both_out, mirror), pair(6)
+    )
+    twin = Exchange(
+        ("slab", half, lambda i: partner),
+        lambda i, to: both_out.at[CORES * i + core],
+        lambda i: both_out.at[CORES * i + core],
+        pair(7),
+    )
+    row = Exchange(along_y, lambda i, to: held, put(mean_out, subject), pair(8))
+    column = Exchange(
+        along_z, lambda i, to: mean_out.at[layer], lambda i: mean_out.at[layer], pair(9)
+    )
+    kept = [
+        pltpu.make_async_copy(mean.at[slab], held.at[slab], own.at[0]),
+        pltpu.make_async_copy(rhs.at[slab], rhs_out.at[slab], own.at[1]),
+        pltpu.make_async_copy(both, both_out.at[slab], own.at[2]),
+        pltpu.make_async_copy(held, mean_out.at[subject], own.at[3]),
     ]
-
-
-def bring_kernel(rhs, both, mean, rhs_out, both_out, mean_out, held, *sems):
-    small = Exchange(mean, held, "slab", sems[0:3])
-    spread = Exchange(held, mean_out, "subj", sems[3:6], whole=True)
-    large = Exchange(rhs, rhs_out, "slab", sems[6:9])
-    shared = Exchange(both, both_out, "slab", sems[9:12], whole=True)
-    greet(("slab", "subj"))
-    small.start()
-    large.start()
-    shared.start()
-    small.wait()
-    spread.start()
-    large.wait()
-    shared.wait()
-    spread.wait()
+    greet(near, far, along_y, along_z)
+    small_far.start()
+    small_near.start()
+    over.start()
+    beside.start()
+    large_near.start()
+    for copy in kept[:3]:
+        copy.start()
+    kept[0].wait()
+    small_near.wait()
+    small_far.wait()
+    row.start()
+    kept[3].start()
+    large_far.start()
+    over.wait()
+    passed.start()
+    kept[3].wait()
+    row.wait()
+    column.start()
+    kept[2].wait()
+    beside.wait()
+    passed.wait()
+    twin.start()
+    kept[1].wait()
+    large_near.wait()
+    twin.wait()
+    large_far.wait()
+    column.wait()
 
 
 def bring(rhs, both, mean):
     slabs, subjects = lax.axis_size("slab"), lax.axis_size("subj")
+    half = slabs // 2
+    x_peers = half // CORES - 1
     vmem = pl.BlockSpec(memory_space=pltpu.VMEM)
     return pl.pallas_call(
         bring_kernel,
@@ -315,34 +378,81 @@
         out_specs=[vmem] * 3,
         scratch_shapes=[
             pltpu.VMEM(mean.shape, jnp.float32),
-            *exchange_sems("slab"),
-            *exchange_sems("subj"),
-            *exchange_sems("slab"),
-            *exchange_sems("slab"),
+            pltpu.SemaphoreType.DMA((4,)),
+            *exchange_sems(half - 1, half, half - 1, half, 1, x_peers, x_peers, half),
+            *exchange_sems(ROW - 1, subjects // ROW - 1),
         ],
         compiler_params=pltpu.CompilerParams(collective_id=0, has_side_effects=True),
         name="bring",
     )(rhs, both, mean)
 
 
-def give_kernel(fields, pieces, fields_out, mean_out, arrived, summed, *sems):
-    parts = Exchange(pieces, arrived, "subj", sems[0:3])
-    large = Exchange(fields, fields_out, "slab", sems[3:6])
-    small = Exchange(summed, mean_out, "slab", sems[6:9])
-    greet(("slab", "subj"))
-    parts.start()
-    large.start()
-    parts.wait()
-    summed[...] = jnp.sum(arrived[...], axis=0)
-    small.start()
-    large.wait()
-    small.wait()
+def give_kernel(
+    fields, pieces, fields_out, mean_out, layers, partial, rows, summed, own, *sems
+):
+    slabs, subjects = fields.shape[0], pieces.shape[0]
+    slab, subject = lax.axis_index("slab"), lax.axis_index("subj")
+    half = slabs // 2
+    y = lax.rem(subject, ROW)
+    z = lax.div(subject, ROW)
+    near = ring("slab", 1, half)
+    far = across("slab", half)
+    along_y = ring("subj", 1, ROW)
+    along_z = ring("subj", ROW, subjects // ROW)
+
+    def pair(k):
+        return sems[2 * k], sems[2 * k + 1]
+
+    def take(ref):
+        return lambda i, to: ref.at[to]
+
+    def put(ref, index):
+        return lambda i: ref.at[index]
+
+    column = Exchange(
+        along_z, lambda i, to: pieces.at[pl.ds(to - y, ROW)], put(layers, z), pair(0)
+    )
+    row = Exchange(
+        along_y, lambda i, to: partial.at[lax.rem(to, ROW)], put(rows, y), pair(1)
+    )
+    large_far = Exchange(far, take(fields), put(fields_out, slab), pair(2))
+    large_near = Exchange(near, take(fields), put(fields_out, slab), pair(3))
+    small_far = Exchange(far, take(summed), put(mean_out, slab), pair(4))
+    small_near = Exchange(near, take(summed), put(mean_out, slab), pair(5))
+    kept = [
+        pltpu.make_async_copy(pieces.at[pl.ds(subject - y, ROW)], layers.at[z], own.at[0]),
+        pltpu.make_async_copy(partial.at[y], rows.at[y], own.at[1]),
+        pltpu.make_async_copy(fields.at[slab], fields_out.at[slab], own.at[2]),
+        pltpu.make_async_copy(summed.at[slab], mean_out.at[slab], own.at[3]),
+    ]
+    greet(near, far, along_y, along_z)
+    column.start()
+    large_far.start()
+    large_near.start()
+    kept[0].start()
+    kept[2].start()
+    kept[0].wait()
+    column.wait()
+    partial[...] = jnp.sum(layers[...], axis=0)
+    row.start()
+    kept[1].start()
+    kept[1].wait()
+    row.wait()
+    summed[...] = jnp.sum(rows[...], axis=0)
+    small_far.start()
+    small_near.start()
+    kept[3].start()
+    for copy in kept[2:]:
+        copy.wait()
+    for exchange in (large_near, large_far, small_near, small_far):
+        exchange.wait()
 
 
 def give(fields, pieces):
-    slabs = lax.axis_size("slab")
+    slabs, subjects = lax.axis_size("slab"), lax.axis_size("subj")
+    half, depth = slabs // 2, subjects // ROW
     vmem = pl.BlockSpec(memory_space=pltpu.VMEM)
-    small = (slabs,) + pieces.shape[2:]
+    small = pieces.shape[1:]
     return pl.pallas_call(
         give_kernel,
         out_shape=[
@@ -352,11 +462,12 @@
         in_specs=[vmem] * 2,
         out_specs=[vmem] * 2,
         scratch_shapes=[
-            pltpu.VMEM(pieces.shape, jnp.float32),
+            pltpu.VMEM((depth, ROW) + small, jnp.float32),
+            pltpu.VMEM((ROW,) + small, jnp.float32),
+            pltpu.VMEM((ROW,) + small, jnp.float32),
             pltpu.VMEM(small, jnp.float32),
-            *exchange_sems("subj"),
-            *exchange_sems("slab"),
-            *exchange_sems("slab"),
+            pltpu.SemaphoreType.DMA((4,)),
+            *exchange_sems(depth - 1, ROW - 1, half, half - 1, half, half - 1),
         ],
         compiler_params=pltpu.CompilerParams(collective_id=1, has_side_effects=True),
         name="give",

time: 113 us -> 94.6 us (0.84)
  Pallas kernels: 106 us -> 87.8 us
    pallas_call x1, Pallas kernels: 57.7 us -> 37.2 us  [bring(): pl.pallas_call(bring_kernel, out_shape=[jax.ShapeDtypeStruct(rhs.shape, j...]
    pallas_call x1, Pallas kernels: 39 us -> 41.4 us  [give(): pl.pallas_call(give_kernel, out_shape=[jax.ShapeDtypeStruct(fields.shape,...]
where the time goes in v4:
time: 94.6 us; the launch traced here: 94.1 us
  Pallas kernels  87.8 us (93%)
  local copies, waits for them, and re-layouts  2.86 us (3%)
  other arithmetic  2.77 us (3%)
    pallas_call x1, Pallas kernels, give(): pl.pallas_call(give_kernel, out_shape=[jax.ShapeDtypeStruct(fields.shape,...  41.4 us
    pallas_call x1, Pallas kernels, bring(): pl.pallas_call(bring_kernel, out_shape=[jax.ShapeDtypeStruct(rhs.shape, j...  37.2 us
    pallas_call x1, Pallas kernels, solve(): pl.pallas_call(solve_kernel, out_shape=[jax.ShapeDtypeStruct(rhs.shape, j...  9.22 us
    unnamed x7, local copies, waits for them, and re-layouts  1.9 us

profile of v4, /device:TPU:1, one launch (start us, length us, event | category | flops | bytes accessed | tf_op | source)
XLA Modules:
  0.0 94.1 jit_solution(4867252936027148481)
XLA Ops:
  0.6 0.1 pad.4.clone
  0.7 0.0 copy-start.2
  0.7 0.8 fusion.2
  1.5 0.0 copy-done.2
  1.5 0.0 copy-start.1
  1.5 0.6 pad_maximum_fusion.both
  2.2 0.1 copy-done.1
  2.3 0.7 maximum_maximum_fusion.mean
  3.0 37.2 %bring.1 = (f32[16,4,1536]{2,1,0:T(4,128)}, f32[16,2,4,1536]{3,2,1,0:T(4,128)}, f32[32,16,2,128]{3,2,1,0:T(2,128)}) custom-call(f32[16,4,1536]{2,1,0:T(4,128)} %bitcast.18, f32[2,4,1536]{2,1,0:T(4,128)} %pad_maximum_fusion.both, f32[16,2,128]{2,1,0:T(2,128)} %maximum_maximum_fusion.mean), custom_call_target="tpu_custom_call" | custom-call | tf_op jit(solution)/shard_map/bring/pallas_call | solution.py:370
  40.2 9.2 %solve.1 = (f32[16,4,1536]{2,1,0:T(4,128)}, f32[32,32,128]{2,1,0:T(8,128)}) custom-call(f32[1,16]{1,0:T(1,128)} %design.1, f32[3,16]{1,0:T(4,128)} %kappa.1, f32[16]{0:T(128)} %scale_ref.1, f32[16,4,1536]{2,1,0:T(4,128)} %get-tuple-element.9.rhs, f32[16,2,4,1536]{3,2,1,0:T(4,128)} %get-tuple-element.10.both, f32[32,32,128]{2,1,0:T(8,128)} %bitcast.17), custom_call_target="tpu_custom_call" | custom-call | tf_op jit(solution)/shard_map/solve/pallas_call | solution.py:208
  49.4 41.4 %give.1 = (f32[16,4,1536]{2,1,0:T(4,128)}, f32[16,2,128]{2,1,0:T(2,128)}) custom-call(f32[16,4,1536]{2,1,0:T(4,128)} %get-tuple-element.12.fields, f32[32,16,2,128]{3,2,1,0:T(2,128)} %bitcast.16), custom_call_target="tpu_custom_call" | custom-call | tf_op jit(solution)/shard_map/give/pallas_call | solution.py:456
  90.8 0.0 copy-start
  90.8 0.9 fusion.4
  91.7 0.0 copy-done
  91.7 0.6 fusion
  92.3 1.8 %copy.13 = f32[1,16,4,1536]{3,2,1,0:T(4,128)} copy(f32[1,16,4,1536]{3,2,1,0:T(4,128)} %bitcast.19) | data formatting | bytes 786432
  (3 shorter events, 0.0 us)
Async XLA Ops:
  0.7 0.8 copy-start.2
  1.5 0.8 copy-start.1
  90.8 0.9 copy-start

commit v5 on v4

--- a/solution.py
+++ b/solution.py
@@ -224,12 +224,22 @@
     return axis, count - 1, lambda i: index + (lax.rem(place + i + 1, count) - place) * stride
 
 
-def across(axis, low):
+def farthest_first(group):
+    axis, peers, peer = group
+    middle = (peers + 1) // 2 - 1
+
+    def ordered(i):
+        return peer(middle + lax.div(i + 1, 2) * (2 * lax.rem(i, 2) - 1))
+
+    return axis, peers, ordered
+
+
+def across(axis, low, first, count):
     index = lax.axis_index(axis)
     place = lax.rem(index, low)
     base = index - place
     other = lax.rem(base + low, 2 * low)
-    return axis, low, lambda i: other + lax.rem(place + i, low)
+    return axis, count, lambda i: other + lax.rem(place + first + i, low)
 
 
 def greet(*groups):
@@ -288,12 +298,17 @@
     half = slabs // 2
     mirror = lax.rem(slab + half, slabs)
     core = lax.rem(slab, CORES)
-    layer = pl.ds(subject - lax.rem(subject, ROW), ROW)
     near = ring("slab", 1, half)
-    far = across("slab", half)
+    far = across("slab", half, 0, half)
+    early = across("slab", half, 0, half // 2)
+    late = across("slab", half, half // 2, half - half // 2)
     along_x = ring("slab", CORES, half // CORES)
     along_y = ring("subj", 1, ROW)
-    along_z = ring("subj", ROW, subjects // ROW)
+    depth = subjects // ROW
+    along_z = ring("subj", ROW, depth)
+    up, down = depth // 2, depth - 1 - depth // 2
+    above, below = along_z[2](0), along_z[2](depth - 2)
+    z = lax.div(subject, ROW)
     partner = ring("slab", 1, CORES)[2](0)
 
     def pair(k):
@@ -308,7 +323,8 @@
     small_near = Exchange(near, take(mean), put(held, slab), pair(0))
     small_far = Exchange(far, take(mean), put(held, slab), pair(1))
     large_near = Exchange(near, take(rhs), put(rhs_out, slab), pair(2))
-    large_far = Exchange(far, take(rhs), put(rhs_out, slab), pair(3))
+    large_early = Exchange(early, take(rhs), put(rhs_out, slab), pair(3))
+    large_late = Exchange(late, take(rhs), put(rhs_out, slab), pair(9))
     over = Exchange(
         ("slab", 1, lambda i: mirror), lambda i, to: both, put(both_out, slab), pair(4)
     )
@@ -323,9 +339,20 @@
         pair(7),
     )
     row = Exchange(along_y, lambda i, to: held, put(mean_out, subject), pair(8))
-    column = Exchange(
-        along_z, lambda i, to: mean_out.at[layer], lambda i: mean_out.at[layer], pair(9)
-    )
+
+    def hop(to, distance, k):
+        layer = mean_out.at[pl.ds(ROW * lax.rem(z + depth + distance, depth), ROW)]
+        return Exchange(("subj", 1, lambda i: to), lambda i, _: layer, lambda i: layer, pair(k))
+
+    ups = [hop(above, -step, 10 + step) for step in range(up)]
+    downs = [hop(below, step, 10 + up + step) for step in range(down)]
+
+    def onward(step):
+        for hops in (ups, downs):
+            if step < len(hops):
+                hops[step - 1].wait()
+                hops[step].start()
+
     kept = [
         pltpu.make_async_copy(mean.at[slab], held.at[slab], own.at[0]),
         pltpu.make_async_copy(rhs.at[slab], rhs_out.at[slab], own.at[1]),
@@ -337,6 +364,7 @@
     small_near.start()
     over.start()
     beside.start()
+    large_early.start()
     large_near.start()
     for copy in kept[:3]:
         copy.start()
@@ -345,21 +373,27 @@
     small_far.wait()
     row.start()
     kept[3].start()
-    large_far.start()
+    large_late.start()
     over.wait()
     passed.start()
     kept[3].wait()
     row.wait()
-    column.start()
+    ups[0].start()
+    downs[0].start()
+    onward(1)
     kept[2].wait()
     beside.wait()
     passed.wait()
     twin.start()
+    for step in range(2, max(up, down)):
+        onward(step)
     kept[1].wait()
     large_near.wait()
     twin.wait()
-    large_far.wait()
-    column.wait()
+    large_early.wait()
+    large_late.wait()
+    ups[-1].wait()
+    downs[-1].wait()
 
 
 def bring(rhs, both, mean):
@@ -379,8 +413,8 @@
         scratch_shapes=[
             pltpu.VMEM(mean.shape, jnp.float32),
             pltpu.SemaphoreType.DMA((4,)),
-            *exchange_sems(half - 1, half, half - 1, half, 1, x_peers, x_peers, half),
-            *exchange_sems(ROW - 1, subjects // ROW - 1),
+            *exchange_sems(half - 1, half, half - 1, half // 2, 1, x_peers, x_peers, half),
+            *exchange_sems(ROW - 1, half - half // 2, *[1] * (subjects // ROW - 1)),
         ],
         compiler_params=pltpu.CompilerParams(collective_id=0, has_side_effects=True),
         name="bring",
@@ -396,9 +430,9 @@
     y = lax.rem(subject, ROW)
     z = lax.div(subject, ROW)
     near = ring("slab", 1, half)
-    far = across("slab", half)
+    far = across("slab", half, 0, half)
     along_y = ring("subj", 1, ROW)
-    along_z = ring("subj", ROW, subjects // ROW)
+    along_z = farthest_first(ring("subj", ROW, subjects // ROW))
 
     def pair(k):
         return sems[2 * k], sems[2 * k + 1]

time: 94.6 us -> 95.5 us (level)
    pallas_call x1, Pallas kernels: 37.2 us -> 40.8 us  [bring(): pl.pallas_call(bring_kernel, out_shape=[jax.ShapeDtypeStruct(rhs.shape, j...]
    pallas_call x1, Pallas kernels: 41.4 us -> 38.6 us  [give(): pl.pallas_call(give_kernel, out_shape=[jax.ShapeDtypeStruct(fields.shape,...]
where the time goes in v5:
time: 95.5 us; the launch traced here: 95 us
  Pallas kernels  88.7 us (93%)
  local copies, waits for them, and re-layouts  2.86 us (3%)
  other arithmetic  2.77 us (3%)
    pallas_call x1, Pallas kernels, bring(): pl.pallas_call(bring_kernel, out_shape=[jax.ShapeDtypeStruct(rhs.shape, j...  40.8 us
    pallas_call x1, Pallas kernels, give(): pl.pallas_call(give_kernel, out_shape=[jax.ShapeDtypeStruct(fields.shape,...  38.6 us
    pallas_call x1, Pallas kernels, solve(): pl.pallas_call(solve_kernel, out_shape=[jax.ShapeDtypeStruct(rhs.shape, j...  9.22 us

profile of v5, /device:TPU:1, one launch (start us, length us, event | category | flops | bytes accessed | tf_op | source)
XLA Modules:
  0.0 95.0 jit_solution(8169270769046248861)
XLA Ops:
  0.6 0.1 pad.4.clone
  0.7 0.0 copy-start.2
  0.7 0.8 fusion.2
  1.5 0.0 copy-done.2
  1.5 0.0 copy-start.1
  1.5 0.6 pad_maximum_fusion.both
  2.2 0.1 copy-done.1
  2.3 0.7 maximum_maximum_fusion.mean
  3.0 40.8 %bring.1 = (f32[16,4,1536]{2,1,0:T(4,128)}, f32[16,2,4,1536]{3,2,1,0:T(4,128)}, f32[32,16,2,128]{3,2,1,0:T(2,128)}) custom-call(f32[16,4,1536]{2,1,0:T(4,128)} %bitcast.18, f32[2,4,1536]{2,1,0:T(4,128)} %pad_maximum_fusion.both, f32[16,2,128]{2,1,0:T(2,128)} %maximum_maximum_fusion.mean), custom_call_target="tpu_custom_call" | custom-call | tf_op jit(solution)/shard_map/bring/pallas_call | solution.py:404
  43.9 9.2 %solve.1 = (f32[16,4,1536]{2,1,0:T(4,128)}, f32[32,32,128]{2,1,0:T(8,128)}) custom-call(f32[1,16]{1,0:T(1,128)} %design.1, f32[3,16]{1,0:T(4,128)} %kappa.1, f32[16]{0:T(128)} %scale_ref.1, f32[16,4,1536]{2,1,0:T(4,128)} %get-tuple-element.9.rhs, f32[16,2,4,1536]{3,2,1,0:T(4,128)} %get-tuple-element.10.both, f32[32,32,128]{2,1,0:T(8,128)} %bitcast.17), custom_call_target="tpu_custom_call" | custom-call | tf_op jit(solution)/shard_map/solve/pallas_call | solution.py:208
  53.1 38.6 %give.1 = (f32[16,4,1536]{2,1,0:T(4,128)}, f32[16,2,128]{2,1,0:T(2,128)}) custom-call(f32[16,4,1536]{2,1,0:T(4,128)} %get-tuple-element.12.fields, f32[32,16,2,128]{3,2,1,0:T(2,128)} %bitcast.16), custom_call_target="tpu_custom_call" | custom-call | tf_op jit(solution)/shard_map/give/pallas_call | solution.py:490
  91.7 0.0 copy-start
  91.7 0.9 fusion.4
  92.6 0.0 copy-done
  92.6 0.6 fusion
  93.2 1.8 %copy.13 = f32[1,16,4,1536]{3,2,1,0:T(4,128)} copy(f32[1,16,4,1536]{3,2,1,0:T(4,128)} %bitcast.19) | data formatting | bytes 786432
  (3 shorter events, 0.0 us)
Async XLA Ops:
  0.7 0.8 copy-start.2
  1.5 0.8 copy-start.1
  91.7 0.9 copy-start

commit v6 on v5

--- a/solution.py
+++ b/solution.py
@@ -242,13 +242,53 @@
     return axis, count, lambda i: other + lax.rem(place + first + i, low)
 
 
+def named(axis, index):
+    return index if isinstance(index, dict) else {axis: index}
+
+
+def turned(half, steps, low):
+    slab, subject = lax.axis_index("slab"), lax.axis_index("subj")
+    y_lo = lax.rem(subject, ROW)
+    y = lax.rem(lax.div(slab, half) * ROW + y_lo + steps, 2 * ROW)
+    return {"subj": subject - y_lo + lax.rem(y, ROW), "slab": lax.div(y, ROW) * half + low}
+
+
+def detour(source, target, passing, sems):
+    half = source.shape[0] // 2
+    count = passing.shape[0]
+    first = half - count
+    back, on = 3 * ROW // 2, ROW // 2
+    slab = lax.axis_index("slab")
+    place = lax.rem(slab, half)
+    base = lax.rem(slab - place + half, 2 * half)
+
+    def low(i):
+        return lax.rem(place + first + i, half)
+
+    out = Exchange(
+        (None, count, lambda i: turned(half, back, place)),
+        lambda i, to: source.at[base + low(i)],
+        lambda i: passing.at[i],
+        sems[0:2],
+    )
+    origin = turned(half, on, place)["slab"]
+    onward = Exchange(
+        (None, count, lambda i: turned(half, back, low(i))),
+        lambda i, to: passing.at[i],
+        lambda i: target.at[origin],
+        sems[2:4],
+    )
+    groups = [(None, half, lambda i, k=k: turned(half, k, i)) for k in (back, on)]
+    return out, onward, groups
+
+
 def greet(*groups):
     barrier = pltpu.get_barrier_semaphore()
     for axis, count, peer in groups:
 
         def signal(i, carry):
             pl.semaphore_signal(
-                barrier, inc=1, device_id={axis: peer(i)}, device_id_type=pl.DeviceIdType.MESH
+                barrier, inc=1, device_id=named(axis, peer(i)), device_id_type=pl.DeviceIdType.MESH
             )
             return carry
 
@@ -269,7 +309,7 @@
             dst_ref=self.target(i),
             send_sem=self.send.at[i],
             recv_sem=self.receive.at[i],
-            device_id={self.axis: to},
+            device_id=named(self.axis, to),
             device_id_type=pl.DeviceIdType.MESH,
         )
 
@@ -292,7 +332,7 @@
     return [pltpu.SemaphoreType.DMA((count,)) for count in counts for _ in range(2)]
 
 
-def bring_kernel(rhs, both, mean, rhs_out, both_out, mean_out, held, own, *sems):
+def bring_kernel(rhs, both, mean, rhs_out, both_out, mean_out, held, passing, own, *sems):
     slabs, subjects = rhs.shape[0], mean_out.shape[0]
     slab, subject = lax.axis_index("slab"), lax.axis_index("subj")
     half = slabs // 2
@@ -301,7 +341,6 @@
     near = ring("slab", 1, half)
     far = across("slab", half, 0, half)
     early = across("slab", half, 0, half // 2)
-    late = across("slab", half, half // 2, half - half // 2)
     along_x = ring("slab", CORES, half // CORES)
     along_y = ring("subj", 1, ROW)
     depth = subjects // ROW
@@ -324,7 +363,7 @@
     small_far = Exchange(far, take(mean), put(held, slab), pair(1))
     large_near = Exchange(near, take(rhs), put(rhs_out, slab), pair(2))
     large_early = Exchange(early, take(rhs), put(rhs_out, slab), pair(3))
-    large_late = Exchange(late, take(rhs), put(rhs_out, slab), pair(9))
+    out, last, around = detour(rhs, rhs_out, passing, sems[-4:])
     over = Exchange(
         ("slab", 1, lambda i: mirror), lambda i, to: both, put(both_out, slab), pair(4)
     )
@@ -344,8 +383,8 @@
         layer = mean_out.at[pl.ds(ROW * lax.rem(z + depth + distance, depth), ROW)]
         return Exchange(("subj", 1, lambda i: to), lambda i, _: layer, lambda i: layer, pair(k))
 
-    ups = [hop(above, -step, 10 + step) for step in range(up)]
-    downs = [hop(below, step, 10 + up + step) for step in range(down)]
+    ups = [hop(above, -step, 9 + step) for step in range(up)]
+    downs = [hop(below, step, 9 + up + step) for step in range(down)]
 
     def onward(step):
         for hops in (ups, downs):
@@ -359,11 +398,12 @@
         pltpu.make_async_copy(both, both_out.at[slab], own.at[2]),
         pltpu.make_async_copy(held, mean_out.at[subject], own.at[3]),
     ]
-    greet(near, far, along_y, along_z)
+    greet(near, far, along_y, along_z, *around)
     small_far.start()
     small_near.start()
     over.start()
     beside.start()
+    out.start()
     large_early.start()
     large_near.start()
     for copy in kept[:3]:
@@ -373,7 +413,6 @@
     small_far.wait()
     row.start()
     kept[3].start()
-    large_late.start()
     over.wait()
     passed.start()
     kept[3].wait()
@@ -385,13 +424,15 @@
     beside.wait()
     passed.wait()
     twin.start()
+    out.wait()
+    last.start()
     for step in range(2, max(up, down)):
         onward(step)
     kept[1].wait()
     large_near.wait()
     twin.wait()
     large_early.wait()
-    large_late.wait()
+    last.wait()
     ups[-1].wait()
     downs[-1].wait()
 
@@ -412,9 +453,10 @@
         out_specs=[vmem] * 3,
         scratch_shapes=[
             pltpu.VMEM(mean.shape, jnp.float32),
+            pltpu.VMEM((half // 2,) + rhs.shape[1:], jnp.float32),
             pltpu.SemaphoreType.DMA((4,)),
             *exchange_sems(half - 1, half, half - 1, half // 2, 1, x_peers, x_peers, half),
-            *exchange_sems(ROW - 1, half - half // 2, *[1] * (subjects // ROW - 1)),
+            *exchange_sems(ROW - 1, *[1] * (subjects // ROW - 1), half // 2, half // 2),
         ],
         compiler_params=pltpu.CompilerParams(collective_id=0, has_side_effects=True),
         name="bring",
@@ -422,7 +464,7 @@
 
 
 def give_kernel(
-    fields, pieces, fields_out, mean_out, layers, partial, rows, summed, own, *sems
+    fields, pieces, fields_out, mean_out, layers, partial, rows, summed, passing, own, *sems
 ):
     slabs, subjects = fields.shape[0], pieces.shape[0]
     slab, subject = lax.axis_index("slab"), lax.axis_index("subj")
@@ -449,7 +491,9 @@
     row = Exchange(
         along_y, lambda i, to: partial.at[lax.rem(to, ROW)], put(rows, y), pair(1)
     )
-    large_far = Exchange(far, take(fields), put(fields_out, slab), pair(2))
+    early = across("slab", half, 0, half // 2)
+    large_far = Exchange(early, take(fields), put(fields_out, slab), pair(2))
+    out, last, around = detour(fields, fields_out, passing, sems[-4:])
     large_near = Exchange(near, take(fields), put(fields_out, slab), pair(3))
     small_far = Exchange(far, take(summed), put(mean_out, slab), pair(4))
     small_near = Exchange(near, take(summed), put(mean_out, slab), pair(5))
@@ -459,13 +503,16 @@
         pltpu.make_async_copy(fields.at[slab], fields_out.at[slab], own.at[2]),
         pltpu.make_async_copy(summed.at[slab], mean_out.at[slab], own.at[3]),
     ]
-    greet(near, far, along_y, along_z)
+    greet(near, far, along_y, along_z, *around)
     column.start()
+    out.start()
     large_far.start()
     large_near.start()
     kept[0].start()
     kept[2].start()
     kept[0].wait()
+    out.wait()
+    last.start()
     column.wait()
     partial[...] = jnp.sum(layers[...], axis=0)
     row.start()
@@ -478,7 +525,7 @@
     kept[3].start()
     for copy in kept[2:]:
         copy.wait()
-    for exchange in (large_near, large_far, small_near, small_far):
+    for exchange in (large_near, large_far, last, small_near, small_far):
         exchange.wait()
 
 
@@ -500,8 +547,10 @@
             pltpu.VMEM((ROW,) + small, jnp.float32),
             pltpu.VMEM((ROW,) + small, jnp.float32),
             pltpu.VMEM(small, jnp.float32),
+            pltpu.VMEM((half // 2,) + fields.shape[1:], jnp.float32),
             pltpu.SemaphoreType.DMA((4,)),
-            *exchange_sems(depth - 1, ROW - 1, half, half - 1, half, half - 1),
+            *exchange_sems(depth - 1, ROW - 1, half // 2, half - 1, half, half - 1),
+            *exchange_sems(half // 2, half // 2),
         ],
         compiler_params=pltpu.CompilerParams(collective_id=1, has_side_effects=True),
         name="give",

time: 95.5 us -> 93.6 us (0.980)
  Pallas kernels: 88.7 us -> 86.8 us
    pallas_call x1, Pallas kernels: 38.6 us -> 33.1 us  [give(): pl.pallas_call(give_kernel, out_shape=[jax.ShapeDtypeStruct(fields.shape,...]
    pallas_call x1, Pallas kernels: 40.8 us -> 44.4 us  [bring(): pl.pallas_call(bring_kernel, out_shape=[jax.ShapeDtypeStruct(rhs.shape, j...]
where the time goes in v6:
time: 93.6 us; the launch traced here: 93.1 us
  Pallas kernels  86.8 us (93%)
  local copies, waits for them, and re-layouts  2.86 us (3%)
  other arithmetic  2.77 us (3%)
    pallas_call x1, Pallas kernels, bring(): pl.pallas_call(bring_kernel, out_shape=[jax.ShapeDtypeStruct(rhs.shape, j...  44.4 us
    pallas_call x1, Pallas kernels, give(): pl.pallas_call(give_kernel, out_shape=[jax.ShapeDtypeStruct(fields.shape,...  33.1 us
    pallas_call x1, Pallas kernels, solve(): pl.pallas_call(solve_kernel, out_shape=[jax.ShapeDtypeStruct(rhs.shape, j...  9.22 us
    unnamed x7, local copies, waits for them, and re-layouts  1.9 us

profile of v6, /device:TPU:1, one launch (start us, length us, event | category | flops | bytes accessed | tf_op | source)
XLA Modules:
  0.0 93.1 jit_solution(11312674052960653999)
XLA Ops:
  0.6 0.1 pad.4.clone
  0.7 0.0 copy-start.2
  0.7 0.8 fusion.2
  1.5 0.0 copy-done.2
  1.5 0.0 copy-start.1
  1.5 0.6 pad_maximum_fusion.both
  2.2 0.1 copy-done.1
  2.3 0.7 maximum_maximum_fusion.mean
  3.0 44.4 %bring.1 = (f32[16,4,1536]{2,1,0:T(4,128)}, f32[16,2,4,1536]{3,2,1,0:T(4,128)}, f32[32,16,2,128]{3,2,1,0:T(2,128)}) custom-call(f32[16,4,1536]{2,1,0:T(4,128)} %bitcast.18, f32[2,4,1536]{2,1,0:T(4,128)} %pad_maximum_fusion.both, f32[16,2,128]{2,1,0:T(2,128)} %maximum_maximum_fusion.mean), custom_call_target="tpu_custom_call" | custom-call | tf_op jit(solution)/shard_map/bring/pallas_call | solution.py:445
  47.4 9.2 %solve.1 = (f32[16,4,1536]{2,1,0:T(4,128)}, f32[32,32,128]{2,1,0:T(8,128)}) custom-call(f32[1,16]{1,0:T(1,128)} %design.1, f32[3,16]{1,0:T(4,128)} %kappa.1, f32[16]{0:T(128)} %scale_ref.1, f32[16,4,1536]{2,1,0:T(4,128)} %get-tuple-element.9.rhs, f32[16,2,4,1536]{3,2,1,0:T(4,128)} %get-tuple-element.10.both, f32[32,32,128]{2,1,0:T(8,128)} %bitcast.17), custom_call_target="tpu_custom_call" | custom-call | tf_op jit(solution)/shard_map/solve/pallas_call | solution.py:208
  56.7 33.1 %give.1 = (f32[16,4,1536]{2,1,0:T(4,128)}, f32[16,2,128]{2,1,0:T(2,128)}) custom-call(f32[16,4,1536]{2,1,0:T(4,128)} %get-tuple-element.12.fields, f32[32,16,2,128]{3,2,1,0:T(2,128)} %bitcast.16), custom_call_target="tpu_custom_call" | custom-call | tf_op jit(solution)/shard_map/give/pallas_call | solution.py:537
  89.8 0.0 copy-start
  89.8 0.9 fusion.4
  90.7 0.0 copy-done
  90.7 0.6 fusion
  91.3 1.8 %copy.13 = f32[1,16,4,1536]{3,2,1,0:T(4,128)} copy(f32[1,16,4,1536]{3,2,1,0:T(4,128)} %bitcast.19) | data formatting | bytes 786432
  (3 shorter events, 0.0 us)
Async XLA Ops:
  0.7 0.8 copy-start.2
  1.5 0.8 copy-start.1
  89.8 0.9 copy-start

commit v7 on v6

--- a/solution.py
+++ b/solution.py
@@ -413,6 +413,8 @@
     small_far.wait()
     row.start()
     kept[3].start()
+    out.wait()
+    last.start()
     over.wait()
     passed.start()
     kept[3].wait()
@@ -424,8 +426,6 @@
     beside.wait()
     passed.wait()
     twin.start()
-    out.wait()
-    last.start()
     for step in range(2, max(up, down)):
         onward(step)
     kept[1].wait()

time: 93.6 us -> 94.6 us (1.011)
  Pallas kernels: 86.8 us -> 87.8 us
    pallas_call x1, Pallas kernels: 33.1 us -> 34.3 us  [give(): pl.pallas_call(give_kernel, out_shape=[jax.ShapeDtypeStruct(fields.shape,...]
where the time goes in v7:
time: 94.6 us; the launch traced here: 94.1 us
  Pallas kernels  87.8 us (93%)
  local copies, waits for them, and re-layouts  2.86 us (3%)
  other arithmetic  2.77 us (3%)
    pallas_call x1, Pallas kernels, bring(): pl.pallas_call(bring_kernel, out_shape=[jax.ShapeDtypeStruct(rhs.shape, j...  44.3 us
    pallas_call x1, Pallas kernels, give(): pl.pallas_call(give_kernel, out_shape=[jax.ShapeDtypeStruct(fields.shape,...  34.3 us
    pallas_call x1, Pallas kernels, solve(): pl.pallas_call(solve_kernel, out_shape=[jax.ShapeDtypeStruct(rhs.shape, j...  9.22 us
    unnamed x7, local copies, waits for them, and re-layouts  1.9 us

profile of v7, /device:TPU:1, one launch (start us, length us, event | category | flops | bytes accessed | tf_op | source)
XLA Modules:
  0.0 94.1 jit_solution(3275609323358664653)
XLA Ops:
  0.6 0.1 pad.4.clone
  0.7 0.0 copy-start.2
  0.7 0.8 fusion.2
  1.5 0.0 copy-done.2
  1.5 0.0 copy-start.1
  1.5 0.6 pad_maximum_fusion.both
  2.2 0.1 copy-done.1
  2.3 0.7 maximum_maximum_fusion.mean
  3.0 44.3 %bring.1 = (f32[16,4,1536]{2,1,0:T(4,128)}, f32[16,2,4,1536]{3,2,1,0:T(4,128)}, f32[32,16,2,128]{3,2,1,0:T(2,128)}) custom-call(f32[16,4,1536]{2,1,0:T(4,128)} %bitcast.18, f32[2,4,1536]{2,1,0:T(4,128)} %pad_maximum_fusion.both, f32[16,2,128]{2,1,0:T(2,128)} %maximum_maximum_fusion.mean), custom_call_target="tpu_custom_call" | custom-call | tf_op jit(solution)/shard_map/bring/pallas_call | solution.py:445
  47.3 9.2 %solve.1 = (f32[16,4,1536]{2,1,0:T(4,128)}, f32[32,32,128]{2,1,0:T(8,128)}) custom-call(f32[1,16]{1,0:T(1,128)} %design.1, f32[3,16]{1,0:T(4,128)} %kappa.1, f32[16]{0:T(128)} %scale_ref.1, f32[16,4,1536]{2,1,0:T(4,128)} %get-tuple-element.9.rhs, f32[16,2,4,1536]{3,2,1,0:T(4,128)} %get-tuple-element.10.both, f32[32,32,128]{2,1,0:T(8,128)} %bitcast.17), custom_call_target="tpu_custom_call" | custom-call | tf_op jit(solution)/shard_map/solve/pallas_call | solution.py:208
  56.5 34.3 %give.1 = (f32[16,4,1536]{2,1,0:T(4,128)}, f32[16,2,128]{2,1,0:T(2,128)}) custom-call(f32[16,4,1536]{2,1,0:T(4,128)} %get-tuple-element.12.fields, f32[32,16,2,128]{3,2,1,0:T(2,128)} %bitcast.16), custom_call_target="tpu_custom_call" | custom-call | tf_op jit(solution)/shard_map/give/pallas_call | solution.py:537
  90.8 0.0 copy-start
  90.8 0.9 fusion.4
  91.7 0.0 copy-done
  91.7 0.6 fusion
  92.4 1.8 %copy.13 = f32[1,16,4,1536]{3,2,1,0:T(4,128)} copy(f32[1,16,4,1536]{3,2,1,0:T(4,128)} %bitcast.19) | data formatting | bytes 786432
  (3 shorter events, 0.0 us)
Async XLA Ops:
  0.7 0.8 copy-start.2
  1.5 0.8 copy-start.1
  90.8 0.9 copy-start
